TPU v7x, 32 devices: a whole 2x2x4 slice. The times are simulated.
32 devices in a mesh: layer: 8 (over z, x), batch: 4 (over y, core).
Axes of the slice: x: 2, y: 2, z: 4, core: 2. Of those that a mesh axis runs over, the one named last changes fastest.
Arguments:
- inputs: float32 [4, 8, 8, 8, 128], P('batch'), parts along dimension 0, may hold values from -6 to 6
- guess_states: float32 [32, 4, 8, 8, 8, 128], P('layer', 'batch'), parts along dimension 1, may hold values from -6 to 6
- kernels: bfloat16 [32, 3, 3, 3, 128, 128], P('layer'), may hold values from -0.109375 to 0.109375
- biases: float32 [32, 128], P('layer'), may hold values from -4 to 4
Outputs:
- states: float32 [32, 4, 8, 8, 8, 128], P('layer', 'batch'), parts along dimension 1
- coarse_residual: float32 [8, 4, 8, 8, 8, 128], P('layer', 'batch'), parts along dimension 1
There are 4 independent parts, one for each index of `batch`. A program takes and returns all parts, laid end to end along the dimension named above; an argument that names none is the same for every part. Nothing has to cross between parts.
All inputs are finite; a program needn't handle non-finite values.
Results may differ from a plain program's by a relative error of at most 0.0008.
Values may be sent and summed in bfloat16 or wider, within the bound.
A program may use at most 128 MiB of HBM per device.

v0:
```python
import jax
import jax.numpy as jnp
from jax import lax
from jax.experimental import pallas as pl
from jax.experimental.pallas import tpu as pltpu
from jax.sharding import PartitionSpec as P

COARSEN = 4
TAPS = 3
MESH = pl.DeviceIdType.MESH


def cycle_kernel(sections, inputs_hbm, guess_ref, kern_ref, bias_hbm, states_ref, residual_ref,
                 inputs_ref, bias_ref,
                 fine_w, lead_w, patches, cur, head, head_mix, first_head, next_head, corner_out,
                 start_in, group_in, top_head, top_rhs, defects, top_in, top_out,
                 load_sem, lead_sem, small_sem, hop_send, hop_recv, w_send, w_recv, sib_send, sib_recv,
                 head_send, head_recv, g_send, g_recv, jump_send, jump_recv):
    depth = guess_ref.shape[0]
    size_x, size_y, size_z, width = inputs_ref.shape
    groups = sections // COARSEN
    fine_size = 2.0 / (depth * sections)
    coarse_size = depth * fine_size
    top_size = COARSEN * coarse_size
    rows = TAPS * TAPS * width
    half_rows = rows // 2
    me = lax.axis_index("layer")
    part = lax.axis_index("batch")
    pos = lax.rem(me, COARSEN)
    group = me // COARSEN
    core = lax.rem(part, 2)
    sibling = part + 1 - 2 * core
    is_first = me == 0
    has_next = me < sections - 1
    has_group_before = group > 0
    has_group_after = group < groups - 1
    span_low = COARSEN // 2
    is_upper = pos >= span_low

    def peer(rel):
        return (group * COARSEN + lax.rem(pos + rel, COARSEN), part)

    def wanted(source, target):
        return jnp.logical_or(target >= span_low, target > source)

    def gives(rel):
        return wanted(pos, lax.rem(pos + rel, COARSEN))

    def takes(rel):
        return wanted(slot_from(rel), pos)

    def slot_from(rel):
        return lax.rem(pos + COARSEN - rel, COARSEN)

    def fine_load(layer, tap):
        return pltpu.make_async_copy(
            kern_ref.at[layer, tap],
            fine_w.at[layer, :, pl.ds(tap * width, width)],
            load_sem.at[layer, tap],
        )

    def lead_load(tap):
        return pltpu.make_async_copy(
            kern_ref.at[0, tap],
            lead_w.at[pos, :, pl.ds(tap * width, width)],
            lead_sem.at[tap],
        )

    inputs_load = pltpu.make_async_copy(inputs_hbm, inputs_ref, small_sem.at[0])
    bias_load = pltpu.make_async_copy(bias_hbm, bias_ref, small_sem.at[1])
    for tap in range(TAPS):
        lead_load(tap).start()
    inputs_load.start()
    bias_load.start()
    for layer in range(depth):
        for tap in range(TAPS):
            fine_load(layer, tap).start()

    barrier = pltpu.get_barrier_semaphore()

    def greet(device):
        pl.semaphore_signal(barrier, inc=1, device_id=device, device_id_type=MESH)

    partners = [(has_next, (me + 1, part)), (me > 0, (me - 1, part)),
                (has_group_after, (me + COARSEN, part)), (has_group_before, (me - COARSEN, part)),
                (jnp.logical_and(is_upper, has_group_after), (me + COARSEN - span_low, part)),
                (jnp.logical_and(pos < span_low, has_group_before), (me - COARSEN + span_low, part))]
    for there, device in partners:
        pl.when(there)(lambda device=device: greet(device))
    for rel in range(1, COARSEN):
        greet(peer(rel))
    greet((me, sibling))
    greetings = sum(jnp.where(there, 1, 0) for there, _ in partners)
    pl.semaphore_wait(barrier, COARSEN + greetings)

    def hop(index, source, target):
        return pltpu.make_async_remote_copy(
            src_ref=source, dst_ref=target, send_sem=hop_send.at[index], recv_sem=hop_recv.at[index],
            device_id=(me + 1, part), device_id_type=MESH)

    first_hop = hop(0, guess_ref.at[depth - 1, 0], first_head)
    second_hop = hop(1, corner_out, next_head)
    pl.when(has_next)(first_hop.start)

    def half(which):
        return pl.ds(pl.multiple_of(which * half_rows, 16), half_rows)

    def w_copy(rel):
        return pltpu.make_async_remote_copy(
            src_ref=lead_w.at[pos, half(core)], dst_ref=lead_w.at[pos, half(core)],
            send_sem=w_send.at[rel], recv_sem=w_recv.at[rel],
            device_id=peer(rel), device_id_type=MESH)

    def w_arrival(rel):
        return pltpu.make_async_remote_copy(
            src_ref=lead_w.at[slot_from(rel), half(core)], dst_ref=lead_w.at[slot_from(rel), half(core)],
            send_sem=w_send.at[rel], recv_sem=w_recv.at[rel],
            device_id=peer(rel), device_id_type=MESH)

    def sib_copy(rel, which):
        return pltpu.make_async_remote_copy(
            src_ref=lead_w.at[slot_from(rel), half(which)], dst_ref=lead_w.at[slot_from(rel), half(which)],
            send_sem=sib_send.at[rel], recv_sem=sib_recv.at[rel],
            device_id=(me, sibling), device_id_type=MESH)

    for tap in range(TAPS):
        lead_load(tap).wait()
    early = (None, pos != 1, pos >= 0, pos == COARSEN - 1)
    for rel in (1, 2, 3):
        pl.when(jnp.logical_and(gives(rel), early[rel]))(w_copy(rel).start)

    z_index = lax.broadcasted_iota(jnp.int32, (size_x * size_y, size_z, width), 1)

    def mix(state, weights):
        squashed = jnp.tanh(state).reshape(size_x * size_y, size_z, width)
        below = jnp.where(z_index == 0, 0.0, pltpu.roll(squashed, 1, 1))
        above = jnp.where(z_index == size_z - 1, 0.0, pltpu.roll(squashed, size_z - 1, 1))
        span = size_y * size_z
        edge = jnp.zeros((size_x, size_z, width), jnp.float32)
        for tap_z, shifted in enumerate((below, squashed, above)):
            shifted = shifted.reshape(size_x, span, width)
            even = shifted.astype(jnp.bfloat16)
            odd = jnp.concatenate([edge, shifted, edge], 1).astype(jnp.bfloat16)
            for tap_y, block in enumerate((odd[:, :span], even, odd[:, 2 * size_z:])):
                column = (tap_y * TAPS + tap_z) * width
                patches[:, :, column:column + width] = block
        left = patches[...].reshape(size_x * span, rows)
        product = jnp.dot(left, weights[...], preferred_element_type=jnp.float32)
        product = product.reshape(size_x, size_y, size_z, TAPS * width)
        plane = jnp.zeros((1, size_y, size_z, width), jnp.float32)
        total = product[..., width:2 * width]
        total = total + jnp.concatenate([plane, product[:-1, :, :, :width]], 0)
        return total + jnp.concatenate([product[1:, :, :, 2 * width:], plane], 0)

    def fine_step(layer):
        state = cur[...]
        mixed = mix(state, fine_w.at[layer])
        return state, mixed, state + fine_size * (mixed + bias_ref[layer])

    pl.when(has_next)(first_hop.wait_send)
    pl.when(me > 0)(first_hop.wait_recv)
    inputs_load.wait()
    bias_load.wait()
    cur[...] = jnp.where(is_first, inputs_ref[...], first_head[...])

    for layer in range(depth):
        for tap in range(TAPS):
            fine_load(layer, tap).wait()

    def sweep_one(layer, carry):
        cur[...] = fine_step(layer)[2]
        return carry

    lax.fori_loop(0, depth, sweep_one, 0)
    corner_out[...] = cur[...]
    pl.when(has_next)(second_hop.start)

    for rel in (1, 2, 3):
        pl.when(jnp.logical_and(gives(rel), jnp.logical_not(early[rel])))(w_copy(rel).start)

    pl.when(has_next)(second_hop.wait_send)
    pl.when(me > 0)(second_hop.wait_recv)

    def head_copy(rel):
        return pltpu.make_async_remote_copy(
            src_ref=next_head, dst_ref=group_in, send_sem=head_send.at[rel], recv_sem=head_recv,
            device_id=peer(rel), device_id_type=MESH)

    leads_group = jnp.logical_and(pos == 0, has_group_before)
    follows = jnp.logical_and(is_upper, has_group_before)
    head[...] = jnp.where(is_first, inputs_ref[...], next_head[...])
    cur[...] = head[...]

    def sweep_two(layer, carry):
        _, mixed, after = fine_step(layer)

        @pl.when(layer == 0)
        def _():
            head_mix[...] = mixed

        cur[...] = after
        return carry

    lax.fori_loop(0, depth, sweep_two, 0)
    defects[pos] = cur[...] - head[...] - coarse_size * head_mix[...]

    def g_copy(rel):
        return pltpu.make_async_remote_copy(
            src_ref=defects.at[pos], dst_ref=defects.at[pos],
            send_sem=g_send.at[rel], recv_sem=g_recv.at[rel], device_id=peer(rel), device_id_type=MESH)

    def g_arrival(rel):
        return pltpu.make_async_remote_copy(
            src_ref=defects.at[slot_from(rel)], dst_ref=defects.at[slot_from(rel)],
            send_sem=g_send.at[rel], recv_sem=g_recv.at[rel], device_id=peer(rel), device_id_type=MESH)

    for rel in range(COARSEN - 1, 0, -1):
        pl.when(gives(rel))(g_copy(rel).start)
    for rel in range(span_low, COARSEN):
        pl.when(leads_group)(head_copy(rel).start)
    for rel in range(1, COARSEN):
        @pl.when(takes(rel))
        def _(rel=rel):
            w_arrival(rel).wait_recv()
            sib_copy(rel, core).start()

    group_in_first = group == 0
    pl.when(follows)(head_copy(1).wait_recv)
    for rel in range(1, COARSEN):
        @pl.when(takes(rel))
        def _(rel=rel):
            sib_copy(rel, 1 - core).wait_recv()

        @pl.when(jnp.logical_and(takes(rel), pos < span_low))
        def _(rel=rel):
            g_arrival(rel).wait_recv()

    def chain(count, arriving=False):
        def step(turn, carry):
            state = cur[...]
            mixed = mix(state, lead_w.at[turn])

            @pl.when(turn == pos)
            def _():
                head[...] = state
                head_mix[...] = mixed

            if arriving:
                rel = lax.rem(pos + COARSEN - turn, COARSEN)
                pl.when(rel > 0)(g_arrival(rel).wait_recv)
            after = state + coarse_size * mixed + defects[turn]
            cur[...] = after
            return carry

        lax.fori_loop(0, count, step, 0)

    def jump(index, source, target, back):
        return pltpu.make_async_remote_copy(
            src_ref=source, dst_ref=target, send_sem=jump_send.at[index], recv_sem=jump_recv.at[min(index, 1)],
            device_id=(me + COARSEN - back, part), device_id_type=MESH)

    relaxed = jump(0, corner_out, start_in, 0)
    solved = jump(1, top_out, top_in, 0)
    solved_low = jump(2, top_out, top_in, span_low)
    upper_sends = jnp.logical_and(is_upper, has_group_after)
    is_owner = pos == COARSEN - 1

    @pl.when(is_upper)
    def _():
        cur[...] = jnp.where(group_in_first, inputs_ref[...], group_in[...])
        chain(COARSEN, arriving=True)
        corner_out[...] = cur[...]
        pl.when(upper_sends)(relaxed.start)
        pl.when(follows)(relaxed.wait_recv)
        start = jnp.where(group_in_first, inputs_ref[...], start_in[...])
        top_head[...] = start

        @pl.when(has_group_before)
        def _():
            cur[...] = start_in[...]
            chain(COARSEN)

        top_w = lead_w.at[COARSEN - 1]
        start = top_head[...]
        top_rhs[...] = cur[...] - start - top_size * mix(start, top_w)
        corner = cur[...]
        residual_ref[0, 0] = jnp.where(is_owner, corner - corner_out[...], corner - corner)
        pl.when(follows)(solved.wait_recv)
        top_head[...] = jnp.where(group_in_first, inputs_ref[...], top_in[...])
        top_out[...] = top_head[...] + top_size * mix(top_head[...], top_w) + top_rhs[...]
        pl.when(upper_sends)(solved.start)
        pl.when(upper_sends)(solved_low.start)

    lower_takes = jnp.logical_and(pos < span_low, has_group_before)
    pl.when(lower_takes)(solved_low.wait_recv)

    @pl.when(pos < span_low)
    def _():
        top_head[...] = jnp.where(group_in_first, inputs_ref[...], top_in[...])

    cur[...] = top_head[...]
    chain(pos + 1)

    @pl.when(pos < span_low)
    def _():
        corner = cur[...]
        residual_ref[0, 0] = corner - corner

    first = head[...] + coarse_size * head_mix[...] + defects[pos]
    states_ref[depth - 1, 0] = jnp.where(is_owner, top_out[...], first)
    cur[...] = head[...] + fine_size * (head_mix[...] + bias_ref[0])
    states_ref[0, 0] = cur[...]

    def last_sweep(layer, carry):
        after = fine_step(layer)[2]
        cur[...] = after
        states_ref[layer, 0] = after
        return carry

    lax.fori_loop(1, depth - 1, last_sweep, 0)

    for rel in range(1, COARSEN):
        pl.when(gives(rel))(w_copy(rel).wait_send)
        pl.when(takes(rel))(sib_copy(rel, core).wait_send)
        pl.when(gives(rel))(g_copy(rel).wait_send)
    for rel in range(span_low, COARSEN):
        pl.when(leads_group)(head_copy(rel).wait_send)
    for copy in (relaxed, solved, solved_low):
        pl.when(upper_sends)(copy.wait_send)


def shards(inputs, guess_states, kernels, biases):
    sections = lax.axis_size("layer")
    depth = guess_states.shape[0]
    state = inputs.shape[1:]
    width = state[-1]
    rows = TAPS * TAPS * width
    vmem = pl.BlockSpec(memory_space=pltpu.VMEM)
    hbm = pl.BlockSpec(memory_space=pltpu.HBM)
    kernel_rows = kernels.reshape(depth, TAPS, rows, width)
    bias_rows = biases.reshape(depth, 1, 1, width)
    f32_state = pltpu.VMEM(state, jnp.float32)
    dma = pltpu.SemaphoreType.DMA

    def body(*refs):
        cycle_kernel(sections, *refs)

    return tuple(pl.pallas_call(
        body,
        name="mgrit_cycle",
        out_shape=(
            jax.ShapeDtypeStruct(guess_states.shape, jnp.float32),
            jax.ShapeDtypeStruct((1,) + guess_states.shape[1:], jnp.float32),
        ),
        in_specs=[hbm, hbm, hbm, hbm],
        out_specs=(vmem, vmem),
        scratch_shapes=[
            f32_state, pltpu.VMEM(bias_rows.shape, jnp.float32),
            pltpu.VMEM((depth, rows, TAPS * width), jnp.bfloat16),
            pltpu.VMEM((COARSEN, rows, TAPS * width), jnp.bfloat16),
            pltpu.VMEM((state[0], state[1] * state[2], rows), jnp.bfloat16),
            f32_state, f32_state, f32_state, f32_state, f32_state, f32_state,
            f32_state, f32_state, f32_state, f32_state,
            pltpu.VMEM((COARSEN,) + state, jnp.float32),
            f32_state, f32_state,
            dma((depth, TAPS)), dma((TAPS,)), dma((2,)), dma((2,)), dma((2,)),
            dma((COARSEN,)), dma((COARSEN,)), dma((COARSEN,)), dma((COARSEN,)),
            dma((COARSEN,)), dma, dma((COARSEN,)), dma((COARSEN,)), dma((3,)), dma((2,)),
        ],
        compiler_params=pltpu.CompilerParams(
            collective_id=0, has_side_effects=True, vmem_limit_bytes=60 * 1024 * 1024),
    )(inputs.reshape(state), guess_states, kernel_rows, bias_rows))


def solution(mesh):
    return jax.shard_map(
        shards,
        mesh=mesh,
        in_specs=(
            P("batch", None, None, None, None),
            P("layer", "batch", None, None, None, None),
            P("layer", None, None, None, None, None),
            P("layer", None),
        ),
        out_specs=(
            P("layer", "batch", None, None, None, None),
            P("layer", "batch", None, None, None, None),
        ),
        check_vma=False,
    )
```

profile of v0, /device:TPU:16, one launch (start us, length us, event | category | flops | bytes accessed | tf_op | source)
XLA Modules:
  0.0 78.9 jit_solution(3423289746186189739)
XLA Ops:
  0.6 74.3 %mgrit_cycle.1 = (f32[4,1,8,8,8,128]{5,4,3,2,1,0:T(8,128)}, f32[1,1,8,8,8,128]{5,4,3,2,1,0:T(8,128)}) custom-call(f32[8,8,8,128]{3,2,1,0:T(8,128)} %bitcast.4, f32[4,1,8,8,8,128]{5,4,3,2,1,0:T(8,128)} %refs_1_.1, bf16[4,3,1152,128]{3,2,1,0:T(8,128)(2,1)} %bitcast.3, f32[4,1,1,128]{3,2,1,0:T(1,128)} %bitcast.5), custom_call_target="tpu_custom_call" | custom-call | tf_op jit(solution)/shard_map/mgrit_cycle/pallas_call | solution.py:348
  75.0 2.3 %copy.8 = f32[4,1,8,8,8,128]{5,4,3,2,1,0:T(8,128)} copy(f32[4,1,8,8,8,128]{5,4,3,2,1,0:T(8,128)} %get-tuple-element.4) | data formatting | bytes 2097152
  77.3 1.7 %copy.9 = f32[1,1,8,8,8,128]{5,4,3,2,1,0:T(8,128)} copy(f32[1,1,8,8,8,128]{5,4,3,2,1,0:T(8,128)} %get-tuple-element.5) | data formatting | bytes 524288
where the time goes:
time: 79.1 us; the launch traced here: 78.9 us
  Pallas kernels  74.3 us (94%)
  local copies, waits for them, and re-layouts  3.98 us (5%)
    pallas_call x1, Pallas kernels, shards(): pl.pallas_call(body, name='mgrit_cycle', out_shape=(jax.ShapeDtypeStruct(...  74.3 us
    unnamed x2, local copies, waits for them, and re-layouts  3.98 us

commit v1 on v0

v1 whole, which is shorter than its diff:
```python
import jax
import jax.numpy as jnp
from jax import lax
from jax.experimental import pallas as pl
from jax.experimental.pallas import tpu as pltpu
from jax.sharding import PartitionSpec as P

COARSEN = 4
TAPS = 3
MESH = pl.DeviceIdType.MESH


def cycle_kernel(sections, inputs_hbm, guess_ref, kern_ref, bias_hbm, states_ref, residual_ref,
                 inputs_ref, bias_ref, fine_w, lead_w, patches, cur, head, head_mix,
                 first_head, next_head, corner_out, seed_out, seed_in, c_point,
                 start_in, top_in, top_out, defects,
                 load_sem, small_sem, hop_send, hop_recv, w_send, w_recv, relay_send, sib_send, sib_recv,
                 g_send, g_recv, seed_send, seed_recv, start_send, start_recv, top_send, top_recv):
    depth = guess_ref.shape[0]
    size_x, size_y, size_z, width = inputs_ref.shape
    groups = sections // COARSEN
    fine_size = 2.0 / (depth * sections)
    coarse_size = depth * fine_size
    top_size = COARSEN * coarse_size
    rows = TAPS * TAPS * width
    half_rows = rows // 2
    last = COARSEN - 1
    me = lax.axis_index("layer")
    part = lax.axis_index("batch")
    pos = lax.rem(me, COARSEN)
    group = me // COARSEN
    core = lax.rem(part, 2)
    sibling = part + 1 - 2 * core
    both = jnp.logical_and
    is_first = me == 0
    has_next = me < sections - 1
    later = group > 0
    has_group_after = group < groups - 1
    is_last_pos = pos == last

    def device(p, ahead=0):
        return ((group + ahead) * COARSEN + p, part)

    barrier = pltpu.get_barrier_semaphore()

    def greet(target):
        pl.semaphore_signal(barrier, inc=1, device_id=target, device_id_type=MESH)

    for rel in range(1, COARSEN):
        greet(device(lax.rem(pos + rel, COARSEN)))
    greet((me, sibling))
    sends_ahead = both(is_last_pos, has_group_after)

    @pl.when(sends_ahead)
    def _():
        for p in range(COARSEN):
            greet(device(p, 1))

    pl.when(later)(lambda: greet(device(last, -1)))

    def fine_load(layer, tap):
        return pltpu.make_async_copy(
            kern_ref.at[layer, tap],
            fine_w.at[layer, :, pl.ds(tap * width, width)],
            load_sem.at[layer, tap],
        )

    inputs_load = pltpu.make_async_copy(inputs_hbm, inputs_ref, small_sem.at[0])
    bias_load = pltpu.make_async_copy(bias_hbm, bias_ref, small_sem.at[1])
    inputs_load.start()
    bias_load.start()
    for layer in range(depth):
        for tap in range(TAPS):
            fine_load(layer, tap).start()

    pl.semaphore_wait(barrier, COARSEN + jnp.where(sends_ahead, COARSEN, 0) + jnp.where(later, 1, 0))

    def remote(source, target, send_sem, recv_sem, where):
        return pltpu.make_async_remote_copy(
            src_ref=source, dst_ref=target, send_sem=send_sem, recv_sem=recv_sem,
            device_id=where, device_id_type=MESH)

    def hop(index, source, target):
        return remote(source, target, hop_send.at[index], hop_recv.at[index], (me + 1, part))

    first_hop = hop(0, guess_ref.at[depth - 1, 0], first_head)
    second_hop = hop(1, corner_out, next_head)
    pl.when(has_next)(first_hop.start)

    half = pl.ds(pl.multiple_of(core * half_rows, 16), half_rows)
    slot = jnp.minimum(pos, last - 1)

    def column(tap):
        return pl.ds(tap * width, width)

    def gives_w(p):
        direct = both(pos < p, jnp.logical_or(later, pos == last - 1))
        return both(direct, pos != 0) if p == last else direct

    def takes(q):
        return both(pos > q, jnp.logical_or(later, q == last - 1))

    def w_copy(p, tap):
        return remote(kern_ref.at[0, tap, half], lead_w.at[slot, half, column(tap)],
                      w_send.at[p, tap], w_recv.at[slot, tap], device(p))

    def w_arrival(q, tap):
        return remote(lead_w.at[q, half, column(tap)], lead_w.at[q, half, column(tap)],
                      w_send.at[0, tap], w_recv.at[q, tap], device(q))

    def relay(tap):
        return remote(lead_w.at[0, half, column(tap)], lead_w.at[0, half, column(tap)],
                      relay_send.at[tap], w_recv.at[0, tap], device(last))

    def sib_copy(q):
        return remote(lead_w.at[q, half], lead_w.at[q, half], sib_send.at[q], sib_recv.at[q], (me, sibling))

    def send_w(taps):
        for tap in taps:
            for p in range(last, 0, -1):
                pl.when(gives_w(p))(w_copy(p, tap).start)

    relays = both(pos == 1, later)

    def send_relay(taps):
        @pl.when(relays)
        def _():
            for tap in taps:
                w_arrival(0, tap).wait_recv()
                relay(tap).start()

    def settle_w(q):
        for tap in range(TAPS):
            arrives = pos != 1 if q == 0 else True
            pl.when(arrives)(w_arrival(q, tap).wait_recv)
        sib_copy(q).start()

    send_w(range(TAPS - 1))

    z_index = lax.broadcasted_iota(jnp.int32, (size_x * size_y, size_z, width), 1)

    def mix(state, weights):
        squashed = jnp.tanh(state).reshape(size_x * size_y, size_z, width)
        below = jnp.where(z_index == 0, 0.0, pltpu.roll(squashed, 1, 1))
        above = jnp.where(z_index == size_z - 1, 0.0, pltpu.roll(squashed, size_z - 1, 1))
        span = size_y * size_z
        edge = jnp.zeros((size_x, size_z, width), jnp.float32)
        for tap_z, shifted in enumerate((below, squashed, above)):
            shifted = shifted.reshape(size_x, span, width)
            even = shifted.astype(jnp.bfloat16)
            odd = jnp.concatenate([edge, shifted, edge], 1).astype(jnp.bfloat16)
            for tap_y, block in enumerate((odd[:, :span], even, odd[:, 2 * size_z:])):
                column = (tap_y * TAPS + tap_z) * width
                patches[:, :, column:column + width] = block
        left = patches[...].reshape(size_x * span, rows)
        product = jnp.dot(left, weights[...], preferred_element_type=jnp.float32)
        product = product.reshape(size_x, size_y, size_z, TAPS * width)
        plane = jnp.zeros((1, size_y, size_z, width), jnp.float32)
        total = product[..., width:2 * width]
        total = total + jnp.concatenate([plane, product[:-1, :, :, :width]], 0)
        return total + jnp.concatenate([product[1:, :, :, 2 * width:], plane], 0)

    def fine_step(layer):
        state = cur[...]
        mixed = mix(state, fine_w.at[layer])
        return state, mixed, state + fine_size * (mixed + bias_ref[layer])

    pl.when(me > 0)(first_hop.wait_recv)
    inputs_load.wait()
    bias_load.wait()
    cur[...] = jnp.where(is_first, inputs_ref[...], first_head[...])

    for layer in range(depth):
        for tap in range(TAPS):
            fine_load(layer, tap).wait()

    def sweep_one(layer, carry):
        after = fine_step(layer)[2]
        cur[...] = after
        states_ref[layer, 0] = after
        return carry

    lax.fori_loop(0, depth, sweep_one, 0)
    corner_out[...] = cur[...]
    pl.when(has_next)(second_hop.start)
    send_w(range(TAPS - 1, TAPS))

    def seed_copy(p):
        return remote(seed_out, seed_in, seed_send.at[p], seed_recv, device(p))

    def gives_seed(p):
        first_group = both(group == 0, pos == 1) if p >= 2 else False
        return jnp.logical_or(first_group, both(later, pos == 0)) if p == last else first_group

    takes_seed = jnp.logical_or(is_last_pos, both(group == 0, pos == 2))

    def g_copy(p):
        return remote(defects.at[pos], defects.at[pos], g_send.at[p], g_recv.at[slot], device(p))

    def g_arrival(q):
        return remote(defects.at[q], defects.at[q], g_send.at[0], g_recv.at[q], device(q))

    def gives_g(p):
        return both(pos < p, jnp.logical_or(later, pos == last - 1))

    @pl.when(me > 0)
    def _():
        second_hop.wait_recv()
        send_relay(range(TAPS - 1))
        head[...] = next_head[...]
        cur[...] = next_head[...]

        def sweep_two(layer, carry):
            _, mixed, after = fine_step(layer)

            @pl.when(layer == 0)
            def _():
                head_mix[...] = mixed

            cur[...] = after
            states_ref[layer, 0] = after
            return carry

        lax.fori_loop(0, depth, sweep_two, 0)
        seed_out[...] = cur[...]
        for p in range(2, COARSEN):
            pl.when(gives_seed(p))(seed_copy(p).start)
        defects[pos] = cur[...] - head[...] - coarse_size * head_mix[...]
        for p in (last, 1, 2):
            pl.when(gives_g(p))(g_copy(p).start)
        send_relay(range(TAPS - 1, TAPS))

    def exchange(qs):
        for q in qs:
            @pl.when(takes(q))
            def _(q=q):
                settle_w(q)
        for q in qs:
            pl.when(takes(q))(sib_copy(q).wait_recv)

    def own_step():
        state = cur[...]
        mixed = mix(state, fine_w.at[0])
        head[...] = state
        head_mix[...] = mixed
        return state + coarse_size * mixed + defects[pos]

    def chain(low, high, arriving=False):
        def step(turn, carry):
            state = cur[...]
            mixed = mix(state, lead_w.at[turn])
            if arriving:
                g_arrival(turn).wait_recv()
            cur[...] = state + coarse_size * mixed + defects[turn]
            return carry

        lax.fori_loop(low, high, step, 0)

    def top_copy(p):
        return remote(top_out, top_in, top_send.at[p], top_recv, device(p, 1))

    def send_top():
        for p in range(last, -1, -1):
            top_copy(p).start()

    start_copy = remote(c_point, start_in, start_send, start_recv, device(last, 1))

    pl.when(takes_seed)(seed_copy(0).wait_recv)

    @pl.when(is_last_pos)
    def _():
        exchange(range(1, last))
        cur[...] = seed_in[...]
        chain(jnp.where(later, 1, 2), last, arriving=True)
        relaxed = own_step()
        c_point[...] = relaxed
        top_out[...] = relaxed
        states_ref[last, 0] = relaxed
        pl.when(both(group == 0, has_group_after))(send_top)
        pl.when(both(later, has_group_after))(start_copy.start)
        exchange(range(1))

    @pl.when(jnp.logical_not(is_last_pos))
    def _():
        exchange(range(last - 1))

    for q in range(last):
        waits = both(takes(q), jnp.logical_not(is_last_pos)) if q > 0 else takes(q)
        pl.when(waits)(g_arrival(q).wait_recv)

    has_start = both(is_last_pos, group > 1)

    @pl.when(has_start)
    def _():
        start_copy.wait_recv()
        cur[...] = start_in[...]
        chain(0, last)
        corner = own_step()
        residual_ref[0, 0] = corner - c_point[...]
        start = start_in[...]
        top_rhs = corner - start - top_size * mix(start, fine_w.at[0])
        top_out[...] = top_rhs

    @pl.when(later)
    def _():
        top_copy(0).wait_recv()

    @pl.when(has_start)
    def _():
        solved = top_in[...]
        top_out[...] = solved + top_size * mix(solved, fine_w.at[0]) + top_out[...]
        pl.when(has_group_after)(send_top)

    steps = jnp.logical_or(later, pos == 2)

    @pl.when(steps)
    def _():
        cur[...] = jnp.where(later, top_in[...], seed_in[...])
        chain(0, jnp.where(later, pos, 0))
        after = own_step()
        states_ref[last, 0] = jnp.where(has_start, top_out[...], after)

        @pl.when(jnp.logical_not(has_start))
        def _():
            residual_ref[0, 0] = after - jnp.where(is_last_pos, c_point[...], after)

        @pl.when(both(is_last_pos, group == 1))
        def _():
            top_out[...] = after
            pl.when(has_group_after)(send_top)

    @pl.when(jnp.logical_not(steps))
    def _():
        corner = states_ref[last, 0]
        residual_ref[0, 0] = corner - corner

    @pl.when(me > 1)
    def _():
        cur[...] = head[...] + fine_size * (head_mix[...] + bias_ref[0])
        states_ref[0, 0] = cur[...]

        def last_sweep(layer, carry):
            after = fine_step(layer)[2]
            cur[...] = after
            states_ref[layer, 0] = after
            return carry

        lax.fori_loop(1, depth - 1, last_sweep, 0)

    pl.when(has_next)(first_hop.wait_send)
    pl.when(has_next)(second_hop.wait_send)
    for p in range(1, COARSEN):
        @pl.when(gives_w(p))
        def _(p=p):
            for tap in range(TAPS):
                w_copy(p, tap).wait_send()

        pl.when(gives_g(p))(g_copy(p).wait_send)
        if p > 1:
            pl.when(gives_seed(p))(seed_copy(p).wait_send)
    for q in range(last):
        pl.when(takes(q))(sib_copy(q).wait_send)

    @pl.when(relays)
    def _():
        for tap in range(TAPS):
            relay(tap).wait_send()

    @pl.when(sends_ahead)
    def _():
        for p in range(COARSEN):
            top_copy(p).wait_send()
        pl.when(later)(start_copy.wait_send)


def shards(inputs, guess_states, kernels, biases):
    sections = lax.axis_size("layer")
    depth = guess_states.shape[0]
    state = inputs.shape[1:]
    width = state[-1]
    rows = TAPS * TAPS * width
    vmem = pl.BlockSpec(memory_space=pltpu.VMEM)
    hbm = pl.BlockSpec(memory_space=pltpu.HBM)
    kernel_rows = kernels.reshape(depth, TAPS, rows, width)
    bias_rows = biases.reshape(depth, 1, 1, width)
    f32_state = pltpu.VMEM(state, jnp.float32)
    dma = pltpu.SemaphoreType.DMA
    operands = [pltpu.with_memory_space_constraint(operand, pltpu.HBM)
                for operand in (inputs.reshape(state), guess_states, kernel_rows, bias_rows)]

    def body(*refs):
        cycle_kernel(sections, *refs)

    return tuple(pl.pallas_call(
        body,
        name="mgrit_cycle",
        out_shape=(
            pltpu.VMEM(guess_states.shape, jnp.float32),
            pltpu.VMEM((1,) + guess_states.shape[1:], jnp.float32),
        ),
        in_specs=[hbm, hbm, hbm, hbm],
        out_specs=(vmem, vmem),
        scratch_shapes=[
            f32_state, pltpu.VMEM(bias_rows.shape, jnp.float32),
            pltpu.VMEM((depth, rows, TAPS * width), jnp.bfloat16),
            pltpu.VMEM((COARSEN - 1, rows, TAPS * width), jnp.bfloat16),
            pltpu.VMEM((state[0], state[1] * state[2], rows), jnp.bfloat16),
            f32_state, f32_state, f32_state, f32_state, f32_state, f32_state,
            f32_state, f32_state, f32_state, f32_state, f32_state, f32_state,
            pltpu.VMEM((COARSEN,) + state, jnp.float32),
            dma((depth, TAPS)), dma((2,)), dma((2,)), dma((2,)),
            dma((COARSEN, TAPS)), dma((COARSEN - 1, TAPS)), dma((TAPS,)),
            dma((COARSEN - 1,)), dma((COARSEN - 1,)),
            dma((COARSEN,)), dma((COARSEN - 1,)), dma((COARSEN,)), dma, dma, dma, dma((COARSEN,)), dma,
        ],
        compiler_params=pltpu.CompilerParams(
            collective_id=0, has_side_effects=True, vmem_limit_bytes=24 * 1024 * 1024),
    )(*operands))


def solution(mesh):
    return jax.shard_map(
        shards,
        mesh=mesh,
        in_specs=(
            P("batch", None, None, None, None),
            P("layer", "batch", None, None, None, None),
            P("layer", None, None, None, None, None),
            P("layer", None),
        ),
        out_specs=(
            P("layer", "batch", None, None, None, None),
            P("layer", "batch", None, None, None, None),
        ),
        check_vma=False,
    )
```

time: 79.1 us -> 75.1 us (0.949)
  the two profiles are of different devices: /device:TPU:16 before, /device:TPU:27 now
where the time goes in v1:
time: 75.1 us; the launch traced here: 75 us
  Pallas kernels  72.7 us (97%)
  local copies, waits for them, and re-layouts  1.67 us (2%)
    pallas_call x1, Pallas kernels, shards(): pl.pallas_call(body, name='mgrit_cycle', out_shape=(pltpu.VMEM(guess_stat...  72.7 us
    unnamed x2, local copies, waits for them, and re-layouts  1.67 us

profile of v1, /device:TPU:27, one launch (start us, length us, event | category | flops | bytes accessed | tf_op | source)
XLA Modules:
  0.0 75.0 jit_solution(5377465729696462393)
XLA Ops:
  0.6 72.7 %mgrit_cycle.1 = (f32[4,1,8,8,8,128]{5,4,3,2,1,0:T(8,128)S(1)}, f32[1,1,8,8,8,128]{5,4,3,2,1,0:T(8,128)S(1)}) custom-call(f32[8,8,8,128]{3,2,1,0:T(8,128)} %bitcast.4, f32[4,1,8,8,8,128]{5,4,3,2,1,0:T(8,128)} %refs_1_.1, bf16[4,3,1152,128]{3,2,1,0:T(8,128)(2,1)} %bitcast.3, f32[4,1,1,128]{3,2,1,0:T(1,128)} %bitcast.5), custom_call_target="tpu_custom_call" | custom-call | tf_op jit(solution)/shard_map/mgrit_cycle/pallas_call | solution.py:394
  73.3 1.0 %copy.8 = f32[4,1,8,8,8,128]{5,4,3,2,1,0:T(8,128)} copy(f32[4,1,8,8,8,128]{5,4,3,2,1,0:T(8,128)S(1)} %get-tuple-element.2) | data formatting | bytes 2097152
  74.3 0.7 copy.9

commit v2 on v1

v2 whole, which is shorter than its diff:
```python
import jax
import jax.numpy as jnp
from jax import lax
from jax.experimental import pallas as pl
from jax.experimental.pallas import tpu as pltpu
from jax.sharding import PartitionSpec as P

COARSEN = 4
TAPS = 3
PIECES = 4
MESH = pl.DeviceIdType.MESH


def cycle_kernel(sections, inputs_hbm, guess_ref, kern_ref, bias_hbm, states_ref, residual_ref,
                 inputs_ref, bias_ref, fine_w, lead_w, patches, cur, head, head_mix,
                 first_head, next_head, corner_out, seed_out, seed_in, c_point,
                 start_in, top_in, top_out, defects,
                 load_sem, small_sem, hop_send, hop_recv, w_send, w_recv, y_send, y_recv, sib_send, sib_recv,
                 extra_send, extra_recv,
                 g_send, g_recv, seed_send, seed_recv, start_send, start_recv, top_send, top_recv):
    depth = guess_ref.shape[0]
    size_x, size_y, size_z, width = inputs_ref.shape
    groups = sections // COARSEN
    fine_size = 2.0 / (depth * sections)
    coarse_size = depth * fine_size
    top_size = COARSEN * coarse_size
    rows = TAPS * TAPS * width
    piece_rows = rows // PIECES
    last = COARSEN - 1
    extra = COARSEN - 2
    me = lax.axis_index("layer")
    part = lax.axis_index("batch")
    pos = lax.rem(me, COARSEN)
    group = me // COARSEN
    core = lax.rem(part, 2)
    row = lax.rem(part // 2, 2)
    sibling = part + 1 - 2 * core
    across = part + 2 - 4 * row
    both = jnp.logical_and
    either = jnp.logical_or
    is_first = me == 0
    has_next = me < sections - 1
    later = group > 0
    opening = group == 0
    has_group_after = group < groups - 1
    is_last_pos = pos == last
    is_upper = pos >= last - 1

    def device(p, ahead=0):
        return ((group + ahead) * COARSEN + p, part)

    barrier = pltpu.get_barrier_semaphore()

    def greet(target):
        pl.semaphore_signal(barrier, inc=1, device_id=target, device_id_type=MESH)

    for rel in range(1, COARSEN):
        greet(device(lax.rem(pos + rel, COARSEN)))
    greet((me, sibling))
    greet((me, across))
    greets_ahead = both(is_upper, has_group_after)

    @pl.when(greets_ahead)
    def _():
        for p in range(COARSEN):
            greet(device(p, 1))

    @pl.when(later)
    def _():
        for p in (last - 1, last):
            greet(device(p, -1))

    def fine_load(layer, tap):
        return pltpu.make_async_copy(
            kern_ref.at[layer, tap],
            fine_w.at[layer, :, pl.ds(tap * width, width)],
            load_sem.at[layer, tap],
        )

    inputs_load = pltpu.make_async_copy(inputs_hbm, inputs_ref, small_sem.at[0])
    bias_load = pltpu.make_async_copy(bias_hbm, bias_ref, small_sem.at[1])
    inputs_load.start()
    bias_load.start()
    for layer in range(depth):
        for tap in range(TAPS):
            fine_load(layer, tap).start()

    greetings = COARSEN + 1 + jnp.where(greets_ahead, COARSEN, 0) + jnp.where(later, 2, 0)
    pl.semaphore_wait(barrier, greetings)

    def remote(source, target, send_sem, recv_sem, where):
        return pltpu.make_async_remote_copy(
            src_ref=source, dst_ref=target, send_sem=send_sem, recv_sem=recv_sem,
            device_id=where, device_id_type=MESH)

    def hop(index, source, target):
        return remote(source, target, hop_send.at[index], hop_recv.at[index], (me + 1, part))

    first_hop = hop(0, guess_ref.at[depth - 1, 0], first_head)
    second_hop = hop(1, corner_out, next_head)
    pl.when(has_next)(first_hop.start)

    slot = jnp.minimum(pos, last - 1)
    quarter = pl.ds(pl.multiple_of((core * 2 + row) * piece_rows, 16), piece_rows)
    half = pl.ds(pl.multiple_of(core * 2 * piece_rows, 16), 2 * piece_rows)

    def w_copy(p):
        return remote(fine_w.at[0, quarter], lead_w.at[slot, quarter], w_send.at[p], w_recv.at[slot], device(p))

    def w_arrival(q):
        return remote(lead_w.at[q, quarter], lead_w.at[q, quarter], w_send.at[0], w_recv.at[q], device(q))

    def y_copy(q):
        return remote(lead_w.at[q, quarter], lead_w.at[q, quarter], y_send.at[q], y_recv.at[q], (me, across))

    def sib_copy(q):
        return remote(lead_w.at[q, half], lead_w.at[q, half], sib_send.at[q], sib_recv.at[q], (me, sibling))

    def extra_copy(index):
        piece = pl.ds(index * piece_rows, piece_rows)
        return remote(fine_w.at[0, piece], lead_w.at[extra, piece], extra_send.at[index], extra_recv.at[index],
                      device(2 * last - 1 - pos))

    gives_extra = both(opening, either(both(pos == last - 1, core == 0), both(pos == last, core == 1)))
    finishes = both(opening, either(both(pos == last, core == 0), both(pos == last - 1, core == 1)))

    def send_w(source, targets):
        @pl.when(both(later, pos == source))
        def _():
            for p in targets:
                w_copy(p).start()

    def send_extra(indices):
        @pl.when(gives_extra)
        def _():
            for index in indices:
                extra_copy(index).start()

    def pass_w(target, qs):
        @pl.when(both(later, pos == target))
        def _():
            for q in qs:
                w_arrival(q).wait_recv()
                y_copy(q).start()

    for tap in range(TAPS):
        fine_load(0, tap).wait()
    send_extra(range(PIECES // 2))
    send_w(0, (1, 2))
    send_w(1, (3,))
    send_w(2, (3,))

    z_index = lax.broadcasted_iota(jnp.int32, (size_x * size_y, size_z, width), 1)

    def mix(state, weights):
        squashed = jnp.tanh(state).reshape(size_x * size_y, size_z, width)
        below = jnp.where(z_index == 0, 0.0, pltpu.roll(squashed, 1, 1))
        above = jnp.where(z_index == size_z - 1, 0.0, pltpu.roll(squashed, size_z - 1, 1))
        span = size_y * size_z
        edge = jnp.zeros((size_x, size_z, width), jnp.float32)
        for tap_z, shifted in enumerate((below, squashed, above)):
            shifted = shifted.reshape(size_x, span, width)
            even = shifted.astype(jnp.bfloat16)
            odd = jnp.concatenate([edge, shifted, edge], 1).astype(jnp.bfloat16)
            for tap_y, block in enumerate((odd[:, :span], even, odd[:, 2 * size_z:])):
                column = (tap_y * TAPS + tap_z) * width
                patches[:, :, column:column + width] = block
        left = patches[...].reshape(size_x * span, rows)
        product = jnp.dot(left, weights[...], preferred_element_type=jnp.float32)
        product = product.reshape(size_x, size_y, size_z, TAPS * width)
        plane = jnp.zeros((1, size_y, size_z, width), jnp.float32)
        total = product[..., width:2 * width]
        total = total + jnp.concatenate([plane, product[:-1, :, :, :width]], 0)
        return total + jnp.concatenate([product[1:, :, :, 2 * width:], plane], 0)

    def fine_step(layer):
        state = cur[...]
        mixed = mix(state, fine_w.at[layer])
        return state, mixed, state + fine_size * (mixed + bias_ref[layer])

    pl.when(me > 0)(first_hop.wait_recv)
    inputs_load.wait()
    bias_load.wait()
    cur[...] = jnp.where(is_first, inputs_ref[...], first_head[...])

    for layer in range(1, depth):
        for tap in range(TAPS):
            fine_load(layer, tap).wait()

    def sweep_one(layer, carry):
        after = fine_step(layer)[2]
        cur[...] = after
        states_ref[layer, 0] = after
        return carry

    lax.fori_loop(0, depth, sweep_one, 0)
    corner_out[...] = cur[...]
    pl.when(has_next)(second_hop.start)
    send_extra(range(PIECES // 2, PIECES))
    send_w(1, (2,))
    pass_w(1, (0,))
    pass_w(2, (0,))
    pass_w(3, (1, 2))

    def seed_copy(p):
        return remote(seed_out, seed_in, seed_send.at[p], seed_recv, device(p))

    def gives_seed(p):
        exact = both(opening, pos == 1)
        if p == last:
            handed = both(opening, both(pos == 2, core == 1))
            return either(both(later, pos == 0), either(both(exact, core == 0), handed))
        return exact

    takes_seed = either(is_last_pos, both(opening, pos == last - 1))

    def g_copy(p):
        return remote(defects.at[pos], defects.at[pos], g_send.at[p], g_recv.at[pos], device(p))

    def g_arrival(q):
        return remote(defects.at[q], defects.at[q], g_send.at[0], g_recv.at[q], device(q))

    def gives_g(p):
        if p == last:
            return both(pos < p, either(later, both(pos == last - 1, core == 0)))
        ahead = both(pos < p, later)
        return either(ahead, both(opening, both(is_last_pos, core == 1))) if p == last - 1 else ahead

    @pl.when(me > 0)
    def _():
        second_hop.wait_recv()
        send_w(0, (3,))
        head[...] = next_head[...]
        cur[...] = next_head[...]

        def sweep_two(layer, carry):
            _, mixed, after = fine_step(layer)

            @pl.when(layer == 0)
            def _():
                head_mix[...] = mixed

            cur[...] = after
            states_ref[layer, 0] = after
            return carry

        lax.fori_loop(0, depth, sweep_two, 0)
        seed_out[...] = cur[...]

        @pl.when(opening)
        def _():
            pl.when(both(gives_seed(last), pos == 1))(seed_copy(last).start)
            pl.when(gives_seed(last - 1))(seed_copy(last - 1).start)

        defects[pos] = cur[...] - head[...] - coarse_size * head_mix[...]
        for p in (last, last - 1, 1):
            pl.when(gives_g(p))(g_copy(p).start)
        pl.when(both(later, gives_seed(last)))(seed_copy(last).start)

    pass_w(2, (1,))
    pass_w(3, (0,))

    for q in range(last):
        @pl.when(both(later, pos > q))
        def _(q=q):
            y_copy(q).wait_recv()
            sib_copy(q).start()

    for q in range(last):
        @pl.when(both(later, pos > q))
        def _(q=q):
            sib_copy(q).wait_recv()
            g_arrival(q).wait_recv()

    def own_step():
        state = cur[...]
        mixed = mix(state, fine_w.at[0])
        head[...] = state
        head_mix[...] = mixed
        return state + coarse_size * mixed + defects[pos]

    def chain(low, high):
        def step(turn, carry):
            state = cur[...]
            cur[...] = state + coarse_size * mix(state, lead_w.at[turn]) + defects[turn]
            return carry

        lax.fori_loop(low, high, step, 0)

    def extra_step(q):
        state = cur[...]
        for index in range(PIECES):
            extra_copy(index).wait_recv()
        mixed = mix(state, lead_w.at[extra])
        g_arrival(q).wait_recv()
        cur[...] = state + coarse_size * mixed + defects[q]

    def top_copy(p):
        return remote(top_out, top_in, top_send.at[p], top_recv, device(p, 1))

    def send_top():
        for p in range(last, -1, -1):
            top_copy(p).start()

    start_copy = remote(c_point, start_in, start_send, start_recv, device(last, 1))

    @pl.when(both(opening, is_upper))
    def _():
        seed_copy(0).wait_recv()
        cur[...] = seed_in[...]

        @pl.when(both(is_last_pos, finishes))
        def _():
            extra_step(last - 1)

        after = own_step()
        states_ref[last, 0] = after
        cur[...] = after

        @pl.when(both(pos == last - 1, finishes))
        def _():
            seed_out[...] = after
            seed_copy(last).start()
            extra_step(last)

        @pl.when(both(finishes, has_group_after))
        def _():
            top_out[...] = cur[...]
            send_top()

    def relax_again():
        seed_copy(0).wait_recv()
        cur[...] = seed_in[...]
        chain(1, last)
        c_point[...] = own_step()

    ends_later = both(is_last_pos, later)

    @pl.when(both(ends_later, has_group_after))
    def _():
        relax_again()
        start_copy.start()

    has_start = both(is_last_pos, group > 1)

    @pl.when(has_start)
    def _():
        start_copy.wait_recv()
        cur[...] = start_in[...]
        chain(0, last)
        corner = own_step()
        residual_ref[0, 0] = corner
        start = start_in[...]
        top_out[...] = corner - start - top_size * mix(start, fine_w.at[0])

    @pl.when(later)
    def _():
        top_copy(0).wait_recv()

    @pl.when(has_start)
    def _():
        solved = top_in[...]
        top_out[...] = solved + top_size * mix(solved, fine_w.at[0]) + top_out[...]
        pl.when(has_group_after)(send_top)

    @pl.when(later)
    def _():
        cur[...] = top_in[...]
        chain(0, pos)
        after = own_step()
        states_ref[last, 0] = jnp.where(has_start, top_out[...], after)

        @pl.when(jnp.logical_not(has_start))
        def _():
            residual_ref[0, 0] = after

        @pl.when(both(both(is_last_pos, group == 1), has_group_after))
        def _():
            top_out[...] = after
            send_top()

    @pl.when(opening)
    def _():
        residual_ref[0, 0] = states_ref[last, 0]

    @pl.when(me > 1)
    def _():
        cur[...] = head[...] + fine_size * (head_mix[...] + bias_ref[0])
        states_ref[0, 0] = cur[...]

        def last_sweep(layer, carry):
            after = fine_step(layer)[2]
            cur[...] = after
            states_ref[layer, 0] = after
            return carry

        lax.fori_loop(1, depth - 1, last_sweep, 0)

    @pl.when(both(ends_later, jnp.logical_not(has_group_after)))
    def _():
        relax_again()

    corner = residual_ref[0, 0]
    residual_ref[0, 0] = corner - jnp.where(ends_later, c_point[...], corner)

    pl.when(has_next)(first_hop.wait_send)
    pl.when(has_next)(second_hop.wait_send)
    for p in range(1, COARSEN):
        pl.when(both(later, pos < p))(w_copy(p).wait_send)
        pl.when(gives_g(p))(g_copy(p).wait_send)
        if p > 1:
            pl.when(gives_seed(p))(seed_copy(p).wait_send)
    for q in range(last):
        pl.when(both(later, pos > q))(y_copy(q).wait_send)
        pl.when(both(later, pos > q))(sib_copy(q).wait_send)

    @pl.when(gives_extra)
    def _():
        for index in range(PIECES):
            extra_copy(index).wait_send()

    @pl.when(both(has_group_after, either(finishes, ends_later)))
    def _():
        for p in range(COARSEN):
            top_copy(p).wait_send()

    pl.when(both(ends_later, has_group_after))(start_copy.wait_send)


def shards(inputs, guess_states, kernels, biases):
    sections = lax.axis_size("layer")
    depth = guess_states.shape[0]
    state = inputs.shape[1:]
    width = state[-1]
    rows = TAPS * TAPS * width
    vmem = pl.BlockSpec(memory_space=pltpu.VMEM)
    hbm = pl.BlockSpec(memory_space=pltpu.HBM)
    kernel_rows = kernels.reshape(depth, TAPS, rows, width)
    bias_rows = biases.reshape(depth, 1, 1, width)
    f32_state = pltpu.VMEM(state, jnp.float32)
    dma = pltpu.SemaphoreType.DMA
    operands = [pltpu.with_memory_space_constraint(operand, pltpu.HBM)
                for operand in (inputs.reshape(state), guess_states, kernel_rows, bias_rows)]

    def body(*refs):
        cycle_kernel(sections, *refs)

    return tuple(pl.pallas_call(
        body,
        name="mgrit_cycle",
        out_shape=(
            pltpu.VMEM(guess_states.shape, jnp.float32),
            pltpu.VMEM((1,) + guess_states.shape[1:], jnp.float32),
        ),
        in_specs=[hbm, hbm, hbm, hbm],
        out_specs=(vmem, vmem),
        scratch_shapes=[
            f32_state, pltpu.VMEM(bias_rows.shape, jnp.float32),
            pltpu.VMEM((depth, rows, TAPS * width), jnp.bfloat16),
            pltpu.VMEM((COARSEN - 1, rows, TAPS * width), jnp.bfloat16),
            pltpu.VMEM((state[0], state[1] * state[2], rows), jnp.bfloat16),
            f32_state, f32_state, f32_state, f32_state, f32_state, f32_state,
            f32_state, f32_state, f32_state, f32_state, f32_state, f32_state,
            pltpu.VMEM((COARSEN,) + state, jnp.float32),
            dma((depth, TAPS)), dma((2,)), dma((2,)), dma((2,)),
            dma((COARSEN,)), dma((COARSEN - 1,)), dma((COARSEN - 1,)), dma((COARSEN - 1,)),
            dma((COARSEN - 1,)), dma((COARSEN - 1,)), dma((PIECES,)), dma((PIECES,)),
            dma((COARSEN,)), dma((COARSEN,)), dma((COARSEN,)), dma, dma, dma, dma((COARSEN,)), dma,
        ],
        compiler_params=pltpu.CompilerParams(
            collective_id=0, has_side_effects=True, vmem_limit_bytes=24 * 1024 * 1024),
    )(*operands))


def solution(mesh):
    return jax.shard_map(
        shards,
        mesh=mesh,
        in_specs=(
            P("batch", None, None, None, None),
            P("layer", "batch", None, None, None, None),
            P("layer", None, None, None, None, None),
            P("layer", None),
        ),
        out_specs=(
            P("layer", "batch", None, None, None, None),
            P("layer", "batch", None, None, None, None),
        ),
        check_vma=False,
    )
```

time: 75.1 us -> 53.2 us (0.71); the launches traced: 75 us -> 52.2 us
  Pallas kernels: 72.7 us -> 49.9 us
    pallas_call x1, Pallas kernels: 72.7 us -> 49.9 us  [shards(): pl.pallas_call(body, name='mgrit_cycle', out_shape=(pltpu.VMEM(guess_stat...]
where the time goes in v2:
time: 53.2 us; the launch traced here: 52.2 us
  Pallas kernels  49.9 us (94%)
  local copies, waits for them, and re-layouts  1.67 us (3%)
  between operations  0.64 us (1%)
    pallas_call x1, Pallas kernels, shards(): pl.pallas_call(body, name='mgrit_cycle', out_shape=(pltpu.VMEM(guess_stat...  49.9 us
    unnamed x2, local copies, waits for them, and re-layouts  1.67 us

profile of v2, /device:TPU:27, one launch (start us, length us, event | category | flops | bytes accessed | tf_op | source)
XLA Modules:
  0.0 52.2 jit_solution(2321995039597569079)
XLA Ops:
  0.6 49.9 %mgrit_cycle.1 = (f32[4,1,8,8,8,128]{5,4,3,2,1,0:T(8,128)S(1)}, f32[1,1,8,8,8,128]{5,4,3,2,1,0:T(8,128)S(1)}) custom-call(f32[8,8,8,128]{3,2,1,0:T(8,128)} %bitcast.4, f32[4,1,8,8,8,128]{5,4,3,2,1,0:T(8,128)} %refs_1_.1, bf16[4,3,1152,128]{3,2,1,0:T(8,128)(2,1)} %bitcast.3, f32[4,1,1,128]{3,2,1,0:T(1,128)} %bitcast.5), custom_call_target="tpu_custom_call" | custom-call | tf_op jit(solution)/shard_map/mgrit_cycle/pallas_call | solution.py:448
  50.5 1.0 %copy.8 = f32[4,1,8,8,8,128]{5,4,3,2,1,0:T(8,128)} copy(f32[4,1,8,8,8,128]{5,4,3,2,1,0:T(8,128)S(1)} %get-tuple-element.2) | data formatting | bytes 2097152
  51.5 0.7 %copy.9 = f32[1,1,8,8,8,128]{5,4,3,2,1,0:T(8,128)} copy(f32[1,1,8,8,8,128]{5,4,3,2,1,0:T(8,128)S(1)} %get-tuple-element.3) | data formatting | bytes 524288

commit v3 on v2

--- a/solution.py
+++ b/solution.py
@@ -16,8 +16,8 @@
                  first_head, next_head, corner_out, seed_out, seed_in, c_point,
                  start_in, top_in, top_out, defects,
                  load_sem, small_sem, hop_send, hop_recv, w_send, w_recv, y_send, y_recv, sib_send, sib_recv,
-                 extra_send, extra_recv,
-                 g_send, g_recv, seed_send, seed_recv, start_send, start_recv, top_send, top_recv):
+                 extra_send, extra_recv, cross_send, cross_recv, gate,
+                 g_send, g_recv, seed_send, seed_recv, origin_send, start_send, start_recv, top_send, top_recv, relay_send, turn_send):
     depth = guess_ref.shape[0]
     size_x, size_y, size_z, width = inputs_ref.shape
     groups = sections // COARSEN
@@ -28,6 +28,7 @@
     piece_rows = rows // PIECES
     last = COARSEN - 1
     extra = COARSEN - 2
+    span = COARSEN // 2
     me = lax.axis_index("layer")
     part = lax.axis_index("batch")
     pos = lax.rem(me, COARSEN)
@@ -98,7 +99,14 @@
 
     first_hop = hop(0, guess_ref.at[depth - 1, 0], first_head)
     second_hop = hop(1, corner_out, next_head)
-    pl.when(has_next)(first_hop.start)
+    staggers = both(has_next, me < 2)
+    leads = both(staggers, core == jnp.where(me == 1, 1, 0))
+    trails = both(staggers, jnp.logical_not(leads))
+    pl.when(both(has_next, jnp.logical_not(trails)))(first_hop.start)
+
+    def open_gate(index):
+        pl.semaphore_signal(gate.at[index], inc=1, device_id=(me, sibling), device_id_type=MESH)
+
 
     slot = jnp.minimum(pos, last - 1)
     quarter = pl.ds(pl.multiple_of((core * 2 + row) * piece_rows, 16), piece_rows)
@@ -110,6 +118,8 @@
     def w_arrival(q):
         return remote(lead_w.at[q, quarter], lead_w.at[q, quarter], w_send.at[0], w_recv.at[q], device(q))
 
+    w_turn = remote(lead_w.at[1, quarter], lead_w.at[1, quarter], turn_send.at[0], w_recv.at[1], device(last - 1))
+
     def y_copy(q):
         return remote(lead_w.at[q, quarter], lead_w.at[q, quarter], y_send.at[q], y_recv.at[q], (me, across))
 
@@ -117,10 +127,15 @@
         return remote(lead_w.at[q, half], lead_w.at[q, half], sib_send.at[q], sib_recv.at[q], (me, sibling))
 
     def extra_copy(index):
-        piece = pl.ds(index * piece_rows, piece_rows)
+        piece = pl.ds(pl.multiple_of((row * 2 + index) * piece_rows, 16), piece_rows)
         return remote(fine_w.at[0, piece], lead_w.at[extra, piece], extra_send.at[index], extra_recv.at[index],
                       device(2 * last - 1 - pos))
 
+    def cross_copy(index):
+        piece = pl.ds(pl.multiple_of((row * 2 + index) * piece_rows, 16), piece_rows)
+        return remote(lead_w.at[extra, piece], lead_w.at[extra, piece], cross_send.at[index], cross_recv.at[index],
+                      (me, across))
+
     gives_extra = both(opening, either(both(pos == last - 1, core == 0), both(pos == last, core == 1)))
     finishes = both(opening, either(both(pos == last, core == 0), both(pos == last - 1, core == 1)))
 
@@ -130,11 +145,25 @@
             for p in targets:
                 w_copy(p).start()
 
-    def send_extra(indices):
-        @pl.when(gives_extra)
-        def _():
-            for index in indices:
+    halves = range(PIECES // 2)
+
+    def send_extra(source):
+        @pl.when(both(gives_extra, pos == source))
+        def _():
+            for index in halves:
                 extra_copy(index).start()
+
+    def pass_extra(target):
+        @pl.when(both(finishes, pos == target))
+        def _():
+            for index in halves:
+                extra_copy(index).wait_recv()
+                cross_copy(index).start()
+
+    def first_wave():
+        send_w(0, (1, 2))
+        send_w(1, (3,))
+        send_w(2, (3,))
 
     def pass_w(target, qs):
         @pl.when(both(later, pos == target))
@@ -142,13 +171,30 @@
             for q in qs:
                 w_arrival(q).wait_recv()
                 y_copy(q).start()
+                if target == last and q == 1:
+                    w_turn.start()
 
     for tap in range(TAPS):
         fine_load(0, tap).wait()
-    send_extra(range(PIECES // 2))
-    send_w(0, (1, 2))
-    send_w(1, (3,))
-    send_w(2, (3,))
+    send_extra(last - 1)
+    inputs_load.wait()
+    bias_load.wait()
+    for layer in range(1, depth):
+        for tap in range(TAPS):
+            fine_load(layer, tap).wait()
+    send_extra(last)
+
+    def let_pass():
+        first_hop.wait_send()
+        open_gate(0)
+
+    def follow():
+        pl.semaphore_wait(gate.at[0], 1)
+        first_hop.start()
+
+    first_wave()
+    pl.when(both(leads, me > 0))(let_pass)
+    pl.when(both(trails, me > 0))(follow)
 
     z_index = lax.broadcasted_iota(jnp.int32, (size_x * size_y, size_z, width), 1)
 
@@ -179,25 +225,23 @@
         return state, mixed, state + fine_size * (mixed + bias_ref[layer])
 
     pl.when(me > 0)(first_hop.wait_recv)
-    inputs_load.wait()
-    bias_load.wait()
     cur[...] = jnp.where(is_first, inputs_ref[...], first_head[...])
-
-    for layer in range(1, depth):
-        for tap in range(TAPS):
-            fine_load(layer, tap).wait()
 
     def sweep_one(layer, carry):
         after = fine_step(layer)[2]
         cur[...] = after
         states_ref[layer, 0] = after
+        pl.when(both(both(leads, is_first), layer == depth - 2))(let_pass)
+        pl.when(both(both(trails, is_first), layer == depth - 2))(follow)
         return carry
 
     lax.fori_loop(0, depth, sweep_one, 0)
     corner_out[...] = cur[...]
     pl.when(has_next)(second_hop.start)
-    send_extra(range(PIECES // 2, PIECES))
-    send_w(1, (2,))
+    origin_copy = remote(corner_out, seed_in, origin_send, seed_recv, device(last, 1))
+    sends_origin = both(is_last_pos, has_group_after)
+    pl.when(sends_origin)(origin_copy.start)
+    pass_extra(last)
     pass_w(1, (0,))
     pass_w(2, (0,))
     pass_w(3, (1, 2))
@@ -209,7 +253,7 @@
         exact = both(opening, pos == 1)
         if p == last:
             handed = both(opening, both(pos == 2, core == 1))
-            return either(both(later, pos == 0), either(both(exact, core == 0), handed))
+            return either(both(exact, core == 0), handed)
         return exact
 
     takes_seed = either(is_last_pos, both(opening, pos == last - 1))
@@ -223,13 +267,14 @@
     def gives_g(p):
         if p == last:
             return both(pos < p, either(later, both(pos == last - 1, core == 0)))
-        ahead = both(pos < p, later)
+        ahead = both(pos < (1 if p == last - 1 else p), later)
         return either(ahead, both(opening, both(is_last_pos, core == 1))) if p == last - 1 else ahead
 
     @pl.when(me > 0)
     def _():
         second_hop.wait_recv()
         send_w(0, (3,))
+        pass_extra(last - 1)
         head[...] = next_head[...]
         cur[...] = next_head[...]
 
@@ -245,20 +290,26 @@
             return carry
 
         lax.fori_loop(0, depth, sweep_two, 0)
-        seed_out[...] = cur[...]
 
         @pl.when(opening)
         def _():
+            seed_out[...] = cur[...]
             pl.when(both(gives_seed(last), pos == 1))(seed_copy(last).start)
-            pl.when(gives_seed(last - 1))(seed_copy(last - 1).start)
+            pl.when(both(gives_seed(last - 1), core == 1))(seed_copy(last - 1).start)
 
         defects[pos] = cur[...] - head[...] - coarse_size * head_mix[...]
         for p in (last, last - 1, 1):
             pl.when(gives_g(p))(g_copy(p).start)
-        pl.when(both(later, gives_seed(last)))(seed_copy(last).start)
+
+    g_turn = remote(defects.at[1], defects.at[1], turn_send.at[1], g_recv.at[1], device(last - 1))
 
     pass_w(2, (1,))
     pass_w(3, (0,))
+
+    @pl.when(both(later, is_last_pos))
+    def _():
+        g_arrival(1).wait_recv()
+        g_turn.start()
 
     for q in range(last):
         @pl.when(both(later, pos > q))
@@ -266,11 +317,15 @@
             y_copy(q).wait_recv()
             sib_copy(q).start()
 
+    ends_later = both(is_last_pos, later)
+    waits_first = both(ends_later, has_group_after)
+
     for q in range(last):
-        @pl.when(both(later, pos > q))
+        @pl.when(both(waits_first, pos > q))
         def _(q=q):
             sib_copy(q).wait_recv()
-            g_arrival(q).wait_recv()
+            if q != 1:
+                g_arrival(q).wait_recv()
 
     def own_step():
         state = cur[...]
@@ -279,28 +334,44 @@
         head_mix[...] = mixed
         return state + coarse_size * mixed + defects[pos]
 
-    def chain(low, high):
+    def chain(low, high, arriving=False):
         def step(turn, carry):
             state = cur[...]
-            cur[...] = state + coarse_size * mix(state, lead_w.at[turn]) + defects[turn]
+            if arriving:
+                pl.when(jnp.logical_not(waits_first))(sib_copy(turn).wait_recv)
+            mixed = mix(state, lead_w.at[turn])
+            if arriving:
+                waits_g = jnp.logical_not(either(waits_first, both(is_last_pos, turn == 1)))
+                pl.when(waits_g)(g_arrival(turn).wait_recv)
+            cur[...] = state + coarse_size * mixed + defects[turn]
             return carry
 
         lax.fori_loop(low, high, step, 0)
 
     def extra_step(q):
         state = cur[...]
-        for index in range(PIECES):
-            extra_copy(index).wait_recv()
+        for index in halves:
+            cross_copy(index).wait_recv()
         mixed = mix(state, lead_w.at[extra])
         g_arrival(q).wait_recv()
         cur[...] = state + coarse_size * mixed + defects[q]
 
-    def top_copy(p):
-        return remote(top_out, top_in, top_send.at[p], top_recv, device(p, 1))
+    half_planes = size_x // 2
+    direct = [(p, h) for p in range(last, -1, -1) for h in range(2) if p >= span or h == 1]
+
+    def top_copy(p, h):
+        planes = pl.ds(h * half_planes, half_planes)
+        return remote(top_out.at[planes], top_in.at[planes], top_send.at[p, h], top_recv.at[h], device(p, 1))
+
+    def top_relay():
+        planes = pl.ds(0, half_planes)
+        return remote(top_in.at[planes], top_in.at[planes], relay_send, top_recv.at[0], device(pos - span))
+
+    relays_top = both(later, pos >= span)
 
     def send_top():
-        for p in range(last, -1, -1):
-            top_copy(p).start()
+        for p, h in direct:
+            top_copy(p, h).start()
 
     start_copy = remote(c_point, start_in, start_send, start_recv, device(last, 1))
 
@@ -331,12 +402,10 @@
     def relax_again():
         seed_copy(0).wait_recv()
         cur[...] = seed_in[...]
-        chain(1, last)
+        chain(0, last)
         c_point[...] = own_step()
 
-    ends_later = both(is_last_pos, later)
-
-    @pl.when(both(ends_later, has_group_after))
+    @pl.when(waits_first)
     def _():
         relax_again()
         start_copy.start()
@@ -355,7 +424,9 @@
 
     @pl.when(later)
     def _():
-        top_copy(0).wait_recv()
+        top_copy(0, 0).wait_recv()
+        pl.when(relays_top)(lambda: top_relay().start())
+        top_copy(0, 1).wait_recv()
 
     @pl.when(has_start)
     def _():
@@ -366,7 +437,7 @@
     @pl.when(later)
     def _():
         cur[...] = top_in[...]
-        chain(0, pos)
+        chain(0, pos, arriving=True)
         after = own_step()
         states_ref[last, 0] = jnp.where(has_start, top_out[...], after)
 
@@ -403,26 +474,51 @@
     corner = residual_ref[0, 0]
     residual_ref[0, 0] = corner - jnp.where(ends_later, c_point[...], corner)
 
-    pl.when(has_next)(first_hop.wait_send)
+    hands_on = both(both(opening, pos == 1), core == 0)
+
+    @pl.when(both(both(opening, pos == 1), core == 1))
+    def _():
+        seed_copy(last - 1).wait_send()
+        open_gate(1)
+
+    @pl.when(hands_on)
+    def _():
+        pl.semaphore_wait(gate.at[1], 1)
+        seed_copy(last - 1).start()
+
+    pl.when(both(has_next, jnp.logical_not(leads)))(first_hop.wait_send)
     pl.when(has_next)(second_hop.wait_send)
     for p in range(1, COARSEN):
-        pl.when(both(later, pos < p))(w_copy(p).wait_send)
+        pl.when(both(later, pos < (1 if p == last - 1 else p)))(w_copy(p).wait_send)
         pl.when(gives_g(p))(g_copy(p).wait_send)
-        if p > 1:
-            pl.when(gives_seed(p))(seed_copy(p).wait_send)
+    pl.when(gives_seed(last))(seed_copy(last).wait_send)
+    pl.when(sends_origin)(origin_copy.wait_send)
+    pl.when(hands_on)(seed_copy(last - 1).wait_send)
     for q in range(last):
         pl.when(both(later, pos > q))(y_copy(q).wait_send)
         pl.when(both(later, pos > q))(sib_copy(q).wait_send)
 
+    @pl.when(ends_later)
+    def _():
+        w_turn.wait_send()
+        g_turn.wait_send()
+
     @pl.when(gives_extra)
     def _():
-        for index in range(PIECES):
+        for index in halves:
             extra_copy(index).wait_send()
 
+    @pl.when(finishes)
+    def _():
+        for index in halves:
+            cross_copy(index).wait_send()
+
     @pl.when(both(has_group_after, either(finishes, ends_later)))
     def _():
-        for p in range(COARSEN):
-            top_copy(p).wait_send()
+        for p, h in direct:
+            top_copy(p, h).wait_send()
+
+    pl.when(relays_top)(lambda: top_relay().wait_send())
 
     pl.when(both(ends_later, has_group_after))(start_copy.wait_send)
 
@@ -464,8 +560,10 @@
             pltpu.VMEM((COARSEN,) + state, jnp.float32),
             dma((depth, TAPS)), dma((2,)), dma((2,)), dma((2,)),
             dma((COARSEN,)), dma((COARSEN - 1,)), dma((COARSEN - 1,)), dma((COARSEN - 1,)),
-            dma((COARSEN - 1,)), dma((COARSEN - 1,)), dma((PIECES,)), dma((PIECES,)),
-            dma((COARSEN,)), dma((COARSEN,)), dma((COARSEN,)), dma, dma, dma, dma((COARSEN,)), dma,
+            dma((COARSEN - 1,)), dma((COARSEN - 1,)), dma((PIECES // 2,)), dma((PIECES // 2,)),
+            dma((PIECES // 2,)), dma((PIECES // 2,)), pltpu.SemaphoreType.REGULAR((2,)),
+            dma((COARSEN,)), dma((COARSEN,)), dma((COARSEN,)), dma, dma, dma, dma,
+            dma((COARSEN, 2)), dma((2,)), dma, dma((2,)),
         ],
         compiler_params=pltpu.CompilerParams(
             collective_id=0, has_side_effects=True, vmem_limit_bytes=24 * 1024 * 1024),

time: 53.2 us -> 51.4 us (0.966)
  the two profiles are of different devices: /device:TPU:27 before, /device:TPU:26 now
where the time goes in v3:
time: 51.4 us; the launch traced here: 51.3 us
  Pallas kernels  49 us (95%)
  local copies, waits for them, and re-layouts  1.67 us (3%)
  between operations  0.64 us (1%)
    pallas_call x1, Pallas kernels, shards(): pl.pallas_call(body, name='mgrit_cycle', out_shape=(pltpu.VMEM(guess_stat...  49 us
    unnamed x2, local copies, waits for them, and re-layouts  1.67 us

profile of v3, /device:TPU:26, one launch (start us, length us, event | category | flops | bytes accessed | tf_op | source)
XLA Modules:
  0.0 51.3 jit_solution(12671939375912671691)
XLA Ops:
  0.6 49.0 %mgrit_cycle.1 = (f32[4,1,8,8,8,128]{5,4,3,2,1,0:T(8,128)S(1)}, f32[1,1,8,8,8,128]{5,4,3,2,1,0:T(8,128)S(1)}) custom-call(f32[8,8,8,128]{3,2,1,0:T(8,128)} %bitcast.4, f32[4,1,8,8,8,128]{5,4,3,2,1,0:T(8,128)} %refs_1_.1, bf16[4,3,1152,128]{3,2,1,0:T(8,128)(2,1)} %bitcast.3, f32[4,1,1,128]{3,2,1,0:T(1,128)} %bitcast.5), custom_call_target="tpu_custom_call" | custom-call | tf_op jit(solution)/shard_map/mgrit_cycle/pallas_call | solution.py:544
  49.6 1.0 %copy.8 = f32[4,1,8,8,8,128]{5,4,3,2,1,0:T(8,128)} copy(f32[4,1,8,8,8,128]{5,4,3,2,1,0:T(8,128)S(1)} %get-tuple-element.2) | data formatting | bytes 2097152
  50.6 0.7 %copy.9 = f32[1,1,8,8,8,128]{5,4,3,2,1,0:T(8,128)} copy(f32[1,1,8,8,8,128]{5,4,3,2,1,0:T(8,128)S(1)} %get-tuple-element.3) | data formatting | bytes 524288

commit v4 on v3

--- a/solution.py
+++ b/solution.py
@@ -17,7 +17,7 @@
                  start_in, top_in, top_out, defects,
                  load_sem, small_sem, hop_send, hop_recv, w_send, w_recv, y_send, y_recv, sib_send, sib_recv,
                  extra_send, extra_recv, cross_send, cross_recv, gate,
-                 g_send, g_recv, seed_send, seed_recv, origin_send, start_send, start_recv, top_send, top_recv, relay_send, turn_send):
+                 g_send, g_recv, seed_send, seed_recv, origin_send, start_send, start_recv, top_send, top_recv, relay_send, turn_send, back_send, ahead_send):
     depth = guess_ref.shape[0]
     size_x, size_y, size_z, width = inputs_ref.shape
     groups = sections // COARSEN
@@ -102,7 +102,8 @@
     staggers = both(has_next, me < 2)
     leads = both(staggers, core == jnp.where(me == 1, 1, 0))
     trails = both(staggers, jnp.logical_not(leads))
-    pl.when(both(has_next, jnp.logical_not(trails)))(first_hop.start)
+    waits_loads = both(core == 1, me > 1)
+    pl.when(both(has_next, jnp.logical_not(either(trails, waits_loads))))(first_hop.start)
 
     def open_gate(index):
         pl.semaphore_signal(gate.at[index], inc=1, device_id=(me, sibling), device_id_type=MESH)
@@ -160,10 +161,22 @@
                 extra_copy(index).wait_recv()
                 cross_copy(index).start()
 
+    w_ahead = remote(lead_w.at[0, quarter], lead_w.at[0, quarter], ahead_send, w_recv.at[0], device(last))
+    back_slot = jnp.maximum(pos - 1, 0)
+    w_back = remote(fine_w.at[0, quarter], lead_w.at[back_slot, quarter], back_send.at[0], w_recv.at[back_slot], device(0))
+
+    def send_back(sources):
+        for source in sources:
+            pl.when(both(later, pos == source))(w_back.start)
+
+    def holds(q):
+        return both(later, either(pos > q, pos == 0))
+
     def first_wave():
-        send_w(0, (1, 2))
+        send_w(0, (2, 1))
         send_w(1, (3,))
         send_w(2, (3,))
+        send_back((1, 2))
 
     def pass_w(target, qs):
         @pl.when(both(later, pos == target))
@@ -182,6 +195,7 @@
     for layer in range(1, depth):
         for tap in range(TAPS):
             fine_load(layer, tap).wait()
+    pl.when(both(has_next, waits_loads))(first_hop.start)
     send_extra(last)
 
     def let_pass():
@@ -238,10 +252,8 @@
     lax.fori_loop(0, depth, sweep_one, 0)
     corner_out[...] = cur[...]
     pl.when(has_next)(second_hop.start)
-    origin_copy = remote(corner_out, seed_in, origin_send, seed_recv, device(last, 1))
-    sends_origin = both(is_last_pos, has_group_after)
-    pl.when(sends_origin)(origin_copy.start)
     pass_extra(last)
+    pass_w(0, (1, 0))
     pass_w(1, (0,))
     pass_w(2, (0,))
     pass_w(3, (1, 2))
@@ -273,7 +285,8 @@
     @pl.when(me > 0)
     def _():
         second_hop.wait_recv()
-        send_w(0, (3,))
+        pl.when(both(later, pos == 1))(w_ahead.start)
+        send_back((3,))
         pass_extra(last - 1)
         head[...] = next_head[...]
         cur[...] = next_head[...]
@@ -303,30 +316,20 @@
 
     g_turn = remote(defects.at[1], defects.at[1], turn_send.at[1], g_recv.at[1], device(last - 1))
 
+    g_back = remote(defects.at[pos], defects.at[pos], back_send.at[1], g_recv.at[pos], device(0))
+    pl.when(both(later, both(pos > 0, pos < last)))(g_back.start)
     pass_w(2, (1,))
     pass_w(3, (0,))
-
-    @pl.when(both(later, is_last_pos))
-    def _():
-        g_arrival(1).wait_recv()
-        g_turn.start()
+    pass_w(0, (2,))
+
 
     for q in range(last):
-        @pl.when(both(later, pos > q))
+        @pl.when(both(later, either(pos > q, both(pos == 0, q < last - 1))))
         def _(q=q):
             y_copy(q).wait_recv()
             sib_copy(q).start()
 
     ends_later = both(is_last_pos, later)
-    waits_first = both(ends_later, has_group_after)
-
-    for q in range(last):
-        @pl.when(both(waits_first, pos > q))
-        def _(q=q):
-            sib_copy(q).wait_recv()
-            if q != 1:
-                g_arrival(q).wait_recv()
-
     def own_step():
         state = cur[...]
         mixed = mix(state, fine_w.at[0])
@@ -338,11 +341,10 @@
         def step(turn, carry):
             state = cur[...]
             if arriving:
-                pl.when(jnp.logical_not(waits_first))(sib_copy(turn).wait_recv)
+                sib_copy(turn).wait_recv()
             mixed = mix(state, lead_w.at[turn])
             if arriving:
-                waits_g = jnp.logical_not(either(waits_first, both(is_last_pos, turn == 1)))
-                pl.when(waits_g)(g_arrival(turn).wait_recv)
+                pl.when(jnp.logical_not(both(is_last_pos, turn == 1)))(g_arrival(turn).wait_recv)
             cur[...] = state + coarse_size * mixed + defects[turn]
             return carry
 
@@ -357,17 +359,23 @@
         cur[...] = state + coarse_size * mixed + defects[q]
 
     half_planes = size_x // 2
-    direct = [(p, h) for p in range(last, -1, -1) for h in range(2) if p >= span or h == 1]
+    direct = [(0, 0), (0, 1), (2, 0), (2, 1), (1, 1)]
+    targets = (last - core, last - span - core, core)
 
     def top_copy(p, h):
         planes = pl.ds(h * half_planes, half_planes)
-        return remote(top_out.at[planes], top_in.at[planes], top_send.at[p, h], top_recv.at[h], device(p, 1))
+        return remote(top_out.at[planes], top_in.at[planes], top_send.at[p, h], top_recv.at[h], device(targets[p], 1))
 
     def top_relay():
         planes = pl.ds(0, half_planes)
-        return remote(top_in.at[planes], top_in.at[planes], relay_send, top_recv.at[0], device(pos - span))
-
-    relays_top = both(later, pos >= span)
+        return remote(top_in.at[planes], top_in.at[planes], relay_send.at[0], top_recv.at[0], device(pos - span))
+
+    def top_side(h):
+        planes = pl.ds(h * half_planes, half_planes)
+        return remote(top_in.at[planes], top_in.at[planes], relay_send.at[h + 1], top_recv.at[h],
+                      device(2 * last - 1 - pos))
+
+    is_primary = both(later, pos == last - core)
 
     def send_top():
         for p, h in direct:
@@ -399,15 +407,41 @@
             top_out[...] = cur[...]
             send_top()
 
-    def relax_again():
-        seed_copy(0).wait_recv()
-        cur[...] = seed_in[...]
-        chain(0, last)
-        c_point[...] = own_step()
-
-    @pl.when(waits_first)
-    def _():
-        relax_again()
+    relaxes = both(later, pos == 0)
+    point_copy = remote(c_point, seed_in, origin_send, seed_recv, device(last))
+
+    @pl.when(relaxes)
+    def _():
+        def step(turn, carry):
+            state = cur[...]
+            sib_copy(turn - 1).wait_recv()
+            mixed = mix(state, lead_w.at[turn - 1])
+
+            @pl.when(turn == last - 1)
+            def _():
+                y_copy(last - 1).wait_recv()
+                sib_copy(last - 1).start()
+
+            after = state + coarse_size * mixed
+
+            @pl.when(turn < last)
+            def _():
+                g_arrival(turn).wait_recv()
+                cur[...] = after + defects[turn]
+
+            @pl.when(turn == last)
+            def _():
+                c_point[...] = after
+
+            return carry
+
+        lax.fori_loop(1, COARSEN, step, 0)
+        point_copy.start()
+
+    @pl.when(both(ends_later, has_group_after))
+    def _():
+        point_copy.wait_recv()
+        c_point[...] = seed_in[...] + defects[last]
         start_copy.start()
 
     has_start = both(is_last_pos, group > 1)
@@ -415,8 +449,10 @@
     @pl.when(has_start)
     def _():
         start_copy.wait_recv()
+        g_arrival(1).wait_recv()
+        g_turn.start()
         cur[...] = start_in[...]
-        chain(0, last)
+        chain(0, last, arriving=True)
         corner = own_step()
         residual_ref[0, 0] = corner
         start = start_in[...]
@@ -425,8 +461,14 @@
     @pl.when(later)
     def _():
         top_copy(0, 0).wait_recv()
-        pl.when(relays_top)(lambda: top_relay().start())
+        pl.when(is_primary)(lambda: (top_side(0).start(), top_relay().start(), None)[-1])
         top_copy(0, 1).wait_recv()
+        pl.when(is_primary)(lambda: top_side(1).start())
+
+        @pl.when(both(is_last_pos, jnp.logical_not(has_start)))
+        def _():
+            g_arrival(1).wait_recv()
+            g_turn.start()
 
     @pl.when(has_start)
     def _():
@@ -437,7 +479,8 @@
     @pl.when(later)
     def _():
         cur[...] = top_in[...]
-        chain(0, pos, arriving=True)
+        pl.when(has_start)(lambda: chain(0, last))
+        pl.when(jnp.logical_not(has_start))(lambda: chain(0, pos, arriving=True))
         after = own_step()
         states_ref[last, 0] = jnp.where(has_start, top_out[...], after)
 
@@ -469,10 +512,10 @@
 
     @pl.when(both(ends_later, jnp.logical_not(has_group_after)))
     def _():
-        relax_again()
+        point_copy.wait_recv()
 
     corner = residual_ref[0, 0]
-    residual_ref[0, 0] = corner - jnp.where(ends_later, c_point[...], corner)
+    residual_ref[0, 0] = corner - jnp.where(ends_later, seed_in[...] + defects[last], corner)
 
     hands_on = both(both(opening, pos == 1), core == 0)
 
@@ -489,14 +532,14 @@
     pl.when(both(has_next, jnp.logical_not(leads)))(first_hop.wait_send)
     pl.when(has_next)(second_hop.wait_send)
     for p in range(1, COARSEN):
-        pl.when(both(later, pos < (1 if p == last - 1 else p)))(w_copy(p).wait_send)
+        sends_w = both(pos > 0, pos < last) if p == last else pos < 1
+        pl.when(both(later, sends_w))(w_copy(p).wait_send)
         pl.when(gives_g(p))(g_copy(p).wait_send)
     pl.when(gives_seed(last))(seed_copy(last).wait_send)
-    pl.when(sends_origin)(origin_copy.wait_send)
     pl.when(hands_on)(seed_copy(last - 1).wait_send)
     for q in range(last):
-        pl.when(both(later, pos > q))(y_copy(q).wait_send)
-        pl.when(both(later, pos > q))(sib_copy(q).wait_send)
+        pl.when(holds(q))(y_copy(q).wait_send)
+        pl.when(holds(q))(sib_copy(q).wait_send)
 
     @pl.when(ends_later)
     def _():
@@ -518,7 +561,22 @@
         for p, h in direct:
             top_copy(p, h).wait_send()
 
-    pl.when(relays_top)(lambda: top_relay().wait_send())
+    @pl.when(is_primary)
+    def _():
+        top_relay().wait_send()
+        top_side(0).wait_send()
+        top_side(1).wait_send()
+
+    pl.when(both(later, pos == 1))(w_ahead.wait_send)
+
+    @pl.when(both(later, pos > 0))
+    def _():
+        w_back.wait_send()
+        pl.when(pos < last)(g_back.wait_send)
+
+    @pl.when(relaxes)
+    def _():
+        point_copy.wait_send()
 
     pl.when(both(ends_later, has_group_after))(start_copy.wait_send)
 
@@ -563,7 +621,7 @@
             dma((COARSEN - 1,)), dma((COARSEN - 1,)), dma((PIECES // 2,)), dma((PIECES // 2,)),
             dma((PIECES // 2,)), dma((PIECES // 2,)), pltpu.SemaphoreType.REGULAR((2,)),
             dma((COARSEN,)), dma((COARSEN,)), dma((COARSEN,)), dma, dma, dma, dma,
-            dma((COARSEN, 2)), dma((2,)), dma, dma((2,)),
+            dma((3, 2)), dma((2,)), dma((3,)), dma((2,)), dma((2,)), dma,
         ],
         compiler_params=pltpu.CompilerParams(
             collective_id=0, has_side_effects=True, vmem_limit_bytes=24 * 1024 * 1024),

time: 51.4 us -> 48.6 us (0.946)
  the two profiles are of different devices: /device:TPU:26 before, /device:TPU:25 now
where the time goes in v4:
time: 48.6 us; the launch traced here: 48.5 us
  Pallas kernels  46.2 us (95%)
  local copies, waits for them, and re-layouts  1.67 us (3%)
  between operations  0.64 us (1%)
    pallas_call x1, Pallas kernels, shards(): pl.pallas_call(body, name='mgrit_cycle', out_shape=(pltpu.VMEM(guess_stat...  46.2 us
    unnamed x2, local copies, waits for them, and re-layouts  1.67 us

profile of v4, /device:TPU:25, one launch (start us, length us, event | category | flops | bytes accessed | tf_op | source)
XLA Modules:
  0.0 48.5 jit_solution(6283614582600919338)
XLA Ops:
  0.6 46.2 %mgrit_cycle.1 = (f32[4,1,8,8,8,128]{5,4,3,2,1,0:T(8,128)S(1)}, f32[1,1,8,8,8,128]{5,4,3,2,1,0:T(8,128)S(1)}) custom-call(f32[8,8,8,128]{3,2,1,0:T(8,128)} %bitcast.4, f32[4,1,8,8,8,128]{5,4,3,2,1,0:T(8,128)} %refs_1_.1, bf16[4,3,1152,128]{3,2,1,0:T(8,128)(2,1)} %bitcast.3, f32[4,1,1,128]{3,2,1,0:T(1,128)} %bitcast.5), custom_call_target="tpu_custom_call" | custom-call | tf_op jit(solution)/shard_map/mgrit_cycle/pallas_call | solution.py:602
  46.8 1.0 %copy.8 = f32[4,1,8,8,8,128]{5,4,3,2,1,0:T(8,128)} copy(f32[4,1,8,8,8,128]{5,4,3,2,1,0:T(8,128)S(1)} %get-tuple-element.2) | data formatting | bytes 2097152
  47.8 0.7 %copy.9 = f32[1,1,8,8,8,128]{5,4,3,2,1,0:T(8,128)} copy(f32[1,1,8,8,8,128]{5,4,3,2,1,0:T(8,128)S(1)} %get-tuple-element.3) | data formatting | bytes 524288

commit v5 on v4

--- a/solution.py
+++ b/solution.py
@@ -460,12 +460,17 @@
 
     @pl.when(later)
     def _():
+        @pl.when(both(jnp.logical_not(is_primary), both(is_last_pos, jnp.logical_not(has_start))))
+        def _():
+            g_arrival(1).wait_recv()
+            g_turn.start()
+
         top_copy(0, 0).wait_recv()
         pl.when(is_primary)(lambda: (top_side(0).start(), top_relay().start(), None)[-1])
         top_copy(0, 1).wait_recv()
         pl.when(is_primary)(lambda: top_side(1).start())
 
-        @pl.when(both(is_last_pos, jnp.logical_not(has_start)))
+        @pl.when(both(is_primary, both(is_last_pos, jnp.logical_not(has_start))))
         def _():
             g_arrival(1).wait_recv()
             g_turn.start()

time: 48.6 us -> 47 us (0.967)
  the two profiles are of different devices: /device:TPU:25 before, /device:TPU:27 now
where the time goes in v5:
time: 47 us; the launch traced here: 46.6 us
  Pallas kernels  44.3 us (94%)
  local copies, waits for them, and re-layouts  1.67 us (4%)
  between operations  0.64 us (1%)
    pallas_call x1, Pallas kernels, shards(): pl.pallas_call(body, name='mgrit_cycle', out_shape=(pltpu.VMEM(guess_stat...  44.3 us
    unnamed x2, local copies, waits for them, and re-layouts  1.67 us

profile of v5, /device:TPU:27, one launch (start us, length us, event | category | flops | bytes accessed | tf_op | source)
XLA Modules:
  0.0 46.6 jit_solution(5812145550267920992)
XLA Ops:
  0.6 44.3 %mgrit_cycle.1 = (f32[4,1,8,8,8,128]{5,4,3,2,1,0:T(8,128)S(1)}, f32[1,1,8,8,8,128]{5,4,3,2,1,0:T(8,128)S(1)}) custom-call(f32[8,8,8,128]{3,2,1,0:T(8,128)} %bitcast.4, f32[4,1,8,8,8,128]{5,4,3,2,1,0:T(8,128)} %refs_1_.1, bf16[4,3,1152,128]{3,2,1,0:T(8,128)(2,1)} %bitcast.3, f32[4,1,1,128]{3,2,1,0:T(1,128)} %bitcast.5), custom_call_target="tpu_custom_call" | custom-call | tf_op jit(solution)/shard_map/mgrit_cycle/pallas_call | solution.py:607
  45.0 1.0 %copy.8 = f32[4,1,8,8,8,128]{5,4,3,2,1,0:T(8,128)} copy(f32[4,1,8,8,8,128]{5,4,3,2,1,0:T(8,128)S(1)} %get-tuple-element.2) | data formatting | bytes 2097152
  45.9 0.7 %copy.9 = f32[1,1,8,8,8,128]{5,4,3,2,1,0:T(8,128)} copy(f32[1,1,8,8,8,128]{5,4,3,2,1,0:T(8,128)S(1)} %get-tuple-element.3) | data formatting | bytes 524288

commit v6 on v5

--- a/solution.py
+++ b/solution.py
@@ -12,10 +12,10 @@
 
 
 def cycle_kernel(sections, inputs_hbm, guess_ref, kern_ref, bias_hbm, states_ref, residual_ref,
-                 inputs_ref, bias_ref, fine_w, lead_w, patches, cur, head, head_mix,
+                 inputs_ref, bias_ref, own_w, fine_w, lead_w, patches, cur, head, head_mix,
                  first_head, next_head, corner_out, seed_out, seed_in, c_point,
                  start_in, top_in, top_out, defects,
-                 load_sem, small_sem, hop_send, hop_recv, w_send, w_recv, y_send, y_recv, sib_send, sib_recv,
+                 own_sem, load_sem, small_sem, hop_send, hop_recv, w_send, w_recv, y_send, y_recv, sib_send, sib_recv,
                  extra_send, extra_recv, cross_send, cross_recv, gate,
                  g_send, g_recv, seed_send, seed_recv, origin_send, start_send, start_recv, top_send, top_recv, relay_send, turn_send, back_send, ahead_send):
     depth = guess_ref.shape[0]
@@ -26,6 +26,8 @@
     top_size = COARSEN * coarse_size
     rows = TAPS * TAPS * width
     piece_rows = rows // PIECES
+    tap_rows = TAPS * width
+    far_rows = 2 * tap_rows
     last = COARSEN - 1
     extra = COARSEN - 2
     span = COARSEN // 2
@@ -71,20 +73,31 @@
         for p in (last - 1, last):
             greet(device(p, -1))
 
-    def fine_load(layer, tap):
+    def own_load(tap):
         return pltpu.make_async_copy(
-            kern_ref.at[layer, tap],
-            fine_w.at[layer, :, pl.ds(tap * width, width)],
-            load_sem.at[layer, tap],
+            kern_ref.at[0, tap], own_w.at[:, pl.ds(tap * width, width)], own_sem.at[tap])
+
+    parts = ((0, 0, rows, 0, 0), (1, 0, rows, 0, width),
+             (2, 0, far_rows, rows, 0), (2, far_rows, tap_rows, rows + tap_rows, width))
+
+    def fine_load(layer, index):
+        tap, start, count, place, column = parts[index]
+        return pltpu.make_async_copy(
+            kern_ref.at[layer, tap, pl.ds(start, count)],
+            fine_w.at[layer - 1, pl.ds(place, count), pl.ds(column, width)],
+            load_sem.at[layer - 1, index],
         )
 
     inputs_load = pltpu.make_async_copy(inputs_hbm, inputs_ref, small_sem.at[0])
     bias_load = pltpu.make_async_copy(bias_hbm, bias_ref, small_sem.at[1])
     inputs_load.start()
     bias_load.start()
-    for layer in range(depth):
-        for tap in range(TAPS):
-            fine_load(layer, tap).start()
+    for tap in range(TAPS):
+        own_load(tap).start()
+    for layer in range(1, depth):
+        for index in range(len(parts)):
+            fine_load(layer, index).start()
+    fine_w[:, rows:rows + tap_rows, width:] = jnp.zeros((depth - 1, tap_rows, width), jnp.bfloat16)
 
     greetings = COARSEN + 1 + jnp.where(greets_ahead, COARSEN, 0) + jnp.where(later, 2, 0)
     pl.semaphore_wait(barrier, greetings)
@@ -114,7 +127,7 @@
     half = pl.ds(pl.multiple_of(core * 2 * piece_rows, 16), 2 * piece_rows)
 
     def w_copy(p):
-        return remote(fine_w.at[0, quarter], lead_w.at[slot, quarter], w_send.at[p], w_recv.at[slot], device(p))
+        return remote(own_w.at[quarter], lead_w.at[slot, quarter], w_send.at[p], w_recv.at[slot], device(p))
 
     def w_arrival(q):
         return remote(lead_w.at[q, quarter], lead_w.at[q, quarter], w_send.at[0], w_recv.at[q], device(q))
@@ -129,7 +142,7 @@
 
     def extra_copy(index):
         piece = pl.ds(pl.multiple_of((row * 2 + index) * piece_rows, 16), piece_rows)
-        return remote(fine_w.at[0, piece], lead_w.at[extra, piece], extra_send.at[index], extra_recv.at[index],
+        return remote(own_w.at[piece], lead_w.at[extra, piece], extra_send.at[index], extra_recv.at[index],
                       device(2 * last - 1 - pos))
 
     def cross_copy(index):
@@ -163,7 +176,7 @@
 
     w_ahead = remote(lead_w.at[0, quarter], lead_w.at[0, quarter], ahead_send, w_recv.at[0], device(last))
     back_slot = jnp.maximum(pos - 1, 0)
-    w_back = remote(fine_w.at[0, quarter], lead_w.at[back_slot, quarter], back_send.at[0], w_recv.at[back_slot], device(0))
+    w_back = remote(own_w.at[quarter], lead_w.at[back_slot, quarter], back_send.at[0], w_recv.at[back_slot], device(0))
 
     def send_back(sources):
         for source in sources:
@@ -188,13 +201,13 @@
                     w_turn.start()
 
     for tap in range(TAPS):
-        fine_load(0, tap).wait()
+        own_load(tap).wait()
     send_extra(last - 1)
     inputs_load.wait()
     bias_load.wait()
     for layer in range(1, depth):
-        for tap in range(TAPS):
-            fine_load(layer, tap).wait()
+        for index in range(len(parts)):
+            fine_load(layer, index).wait()
     pl.when(both(has_next, waits_loads))(first_hop.start)
     send_extra(last)
 
@@ -212,7 +225,7 @@
 
     z_index = lax.broadcasted_iota(jnp.int32, (size_x * size_y, size_z, width), 1)
 
-    def mix(state, weights):
+    def gather(state):
         squashed = jnp.tanh(state).reshape(size_x * size_y, size_z, width)
         below = jnp.where(z_index == 0, 0.0, pltpu.roll(squashed, 1, 1))
         above = jnp.where(z_index == size_z - 1, 0.0, pltpu.roll(squashed, size_z - 1, 1))
@@ -225,7 +238,10 @@
             for tap_y, block in enumerate((odd[:, :span], even, odd[:, 2 * size_z:])):
                 column = (tap_y * TAPS + tap_z) * width
                 patches[:, :, column:column + width] = block
-        left = patches[...].reshape(size_x * span, rows)
+        return patches[...].reshape(size_x * span, rows)
+
+    def mix(state, weights):
+        left = gather(state)
         product = jnp.dot(left, weights[...], preferred_element_type=jnp.float32)
         product = product.reshape(size_x, size_y, size_z, TAPS * width)
         plane = jnp.zeros((1, size_y, size_z, width), jnp.float32)
@@ -233,23 +249,37 @@
         total = total + jnp.concatenate([plane, product[:-1, :, :, :width]], 0)
         return total + jnp.concatenate([product[1:, :, :, 2 * width:], plane], 0)
 
-    def fine_step(layer):
+    def packed_mix(state, weights):
+        left = gather(state)
+        near = jnp.dot(left, weights[:rows], preferred_element_type=jnp.float32)
+        far = jnp.dot(left[:, :far_rows], weights[rows:], preferred_element_type=jnp.float32)
+        near = near.reshape(size_x, size_y, size_z, 2 * width)
+        far = far.reshape(size_x, size_y, size_z, 2 * width)
+        plane = jnp.zeros((1, size_y, size_z, width), jnp.float32)
+        line = jnp.zeros((size_x - 1, 1, size_z, width), jnp.float32)
+        ahead = far[1:, :, :, :width] + jnp.concatenate([far[1:, 1:, :, width:], line], 1)
+        total = near[..., width:]
+        total = total + jnp.concatenate([plane, near[:-1, :, :, :width]], 0)
+        return total + jnp.concatenate([ahead, plane], 0)
+
+    def fine_step(layer, lead=False):
         state = cur[...]
-        mixed = mix(state, fine_w.at[layer])
+        mixed = mix(state, own_w) if lead else packed_mix(state, fine_w.at[layer - 1])
         return state, mixed, state + fine_size * (mixed + bias_ref[layer])
 
     pl.when(me > 0)(first_hop.wait_recv)
     cur[...] = jnp.where(is_first, inputs_ref[...], first_head[...])
 
-    def sweep_one(layer, carry):
-        after = fine_step(layer)[2]
+    def sweep_one(layer, carry, lead=False):
+        after = fine_step(layer, lead)[2]
         cur[...] = after
         states_ref[layer, 0] = after
         pl.when(both(both(leads, is_first), layer == depth - 2))(let_pass)
         pl.when(both(both(trails, is_first), layer == depth - 2))(follow)
         return carry
 
-    lax.fori_loop(0, depth, sweep_one, 0)
+    sweep_one(0, 0, True)
+    lax.fori_loop(1, depth, sweep_one, 0)
     corner_out[...] = cur[...]
     pl.when(has_next)(second_hop.start)
     pass_extra(last)
@@ -291,18 +321,16 @@
         head[...] = next_head[...]
         cur[...] = next_head[...]
 
-        def sweep_two(layer, carry):
-            _, mixed, after = fine_step(layer)
-
-            @pl.when(layer == 0)
-            def _():
+        def sweep_two(layer, carry, lead=False):
+            _, mixed, after = fine_step(layer, lead)
+            if lead:
                 head_mix[...] = mixed
-
             cur[...] = after
             states_ref[layer, 0] = after
             return carry
 
-        lax.fori_loop(0, depth, sweep_two, 0)
+        sweep_two(0, 0, True)
+        lax.fori_loop(1, depth, sweep_two, 0)
 
         @pl.when(opening)
         def _():
@@ -332,7 +360,7 @@
     ends_later = both(is_last_pos, later)
     def own_step():
         state = cur[...]
-        mixed = mix(state, fine_w.at[0])
+        mixed = mix(state, own_w)
         head[...] = state
         head_mix[...] = mixed
         return state + coarse_size * mixed + defects[pos]
@@ -456,7 +484,7 @@
         corner = own_step()
         residual_ref[0, 0] = corner
         start = start_in[...]
-        top_out[...] = corner - start - top_size * mix(start, fine_w.at[0])
+        top_out[...] = corner - start - top_size * mix(start, own_w)
 
     @pl.when(later)
     def _():
@@ -478,7 +506,7 @@
     @pl.when(has_start)
     def _():
         solved = top_in[...]
-        top_out[...] = solved + top_size * mix(solved, fine_w.at[0]) + top_out[...]
+        top_out[...] = solved + top_size * mix(solved, own_w) + top_out[...]
         pl.when(has_group_after)(send_top)
 
     @pl.when(later)
@@ -604,7 +632,7 @@
     def body(*refs):
         cycle_kernel(sections, *refs)
 
-    return tuple(pl.pallas_call(
+    kept = pl.pallas_call(
         body,
         name="mgrit_cycle",
         out_shape=(
@@ -615,13 +643,14 @@
         out_specs=(vmem, vmem),
         scratch_shapes=[
             f32_state, pltpu.VMEM(bias_rows.shape, jnp.float32),
-            pltpu.VMEM((depth, rows, TAPS * width), jnp.bfloat16),
+            pltpu.VMEM((rows, TAPS * width), jnp.bfloat16),
+            pltpu.VMEM((depth - 1, rows + 2 * TAPS * width, 2 * width), jnp.bfloat16),
             pltpu.VMEM((COARSEN - 1, rows, TAPS * width), jnp.bfloat16),
             pltpu.VMEM((state[0], state[1] * state[2], rows), jnp.bfloat16),
             f32_state, f32_state, f32_state, f32_state, f32_state, f32_state,
             f32_state, f32_state, f32_state, f32_state, f32_state, f32_state,
             pltpu.VMEM((COARSEN,) + state, jnp.float32),
-            dma((depth, TAPS)), dma((2,)), dma((2,)), dma((2,)),
+            dma((TAPS,)), dma((depth - 1, TAPS + 1)), dma((2,)), dma((2,)), dma((2,)),
             dma((COARSEN,)), dma((COARSEN - 1,)), dma((COARSEN - 1,)), dma((COARSEN - 1,)),
             dma((COARSEN - 1,)), dma((COARSEN - 1,)), dma((PIECES // 2,)), dma((PIECES // 2,)),
             dma((PIECES // 2,)), dma((PIECES // 2,)), pltpu.SemaphoreType.REGULAR((2,)),
@@ -630,7 +659,25 @@
         ],
         compiler_params=pltpu.CompilerParams(
             collective_id=0, has_side_effects=True, vmem_limit_bytes=24 * 1024 * 1024),
-    )(*operands))
+    )(*operands)
+
+    def flush(states_ref, residual_ref, states_out, residual_out, sem):
+        copies = [pltpu.make_async_copy(source, target, sem.at[index])
+                  for index, (source, target) in enumerate(((states_ref, states_out), (residual_ref, residual_out)))]
+        for copy in copies:
+            copy.start()
+        for copy in copies:
+            copy.wait()
+
+    return tuple(pl.pallas_call(
+        flush,
+        name="flush",
+        out_shape=tuple(jax.ShapeDtypeStruct(array.shape, jnp.float32) for array in kept),
+        in_specs=[vmem, vmem],
+        out_specs=(hbm, hbm),
+        scratch_shapes=[dma((2,))],
+        compiler_params=pltpu.CompilerParams(vmem_limit_bytes=4 * 1024 * 1024),
+    )(*[pltpu.with_memory_space_constraint(array, pltpu.VMEM) for array in kept]))
 
 
 def solution(mesh):

time: 47 us -> 45.9 us (0.977)
  local copies, waits for them, and re-layouts: 1.67 us -> 0 us
  Pallas kernels: 44.3 us -> 45.1 us
    unnamed x2 -> x0, local copies, waits for them, and re-layouts: 1.67 us -> none
    pallas_call x0 -> x1, Pallas kernels: none -> 1.07 us  [shards(): pl.pallas_call(flush, name='flush', out_shape=tuple((jax.ShapeDtypeStruct...]
where the time goes in v6:
time: 45.9 us; the launch traced here: 45.8 us
  Pallas kernels  45.1 us (98%)
  between operations  0.64 us (1%)
    pallas_call x1, Pallas kernels, shards(): pl.pallas_call(body, name='mgrit_cycle', out_shape=(pltpu.VMEM(guess_stat...  44.1 us
    pallas_call x1, Pallas kernels, shards(): pl.pallas_call(flush, name='flush', out_shape=tuple((jax.ShapeDtypeStruct...  1.07 us

profile of v6, /device:TPU:27, one launch (start us, length us, event | category | flops | bytes accessed | tf_op | source)
XLA Modules:
  0.0 45.8 jit_solution(9274086675254599882)
XLA Ops:
  0.6 44.1 %mgrit_cycle.1 = (f32[4,1,8,8,8,128]{5,4,3,2,1,0:T(8,128)S(1)}, f32[1,1,8,8,8,128]{5,4,3,2,1,0:T(8,128)S(1)}) custom-call(f32[8,8,8,128]{3,2,1,0:T(8,128)} %bitcast.4, f32[4,1,8,8,8,128]{5,4,3,2,1,0:T(8,128)} %refs_1_.1, bf16[4,3,1152,128]{3,2,1,0:T(8,128)(2,1)} %bitcast.3, f32[4,1,1,128]{3,2,1,0:T(1,128)} %bitcast.5), custom_call_target="tpu_custom_call" | custom-call | tf_op jit(solution)/shard_map/mgrit_cycle/pallas_call | solution.py:635
  44.7 1.1 %flush.1 = (f32[4,1,8,8,8,128]{5,4,3,2,1,0:T(8,128)}, f32[1,1,8,8,8,128]{5,4,3,2,1,0:T(8,128)}) custom-call(f32[4,1,8,8,8,128]{5,4,3,2,1,0:T(8,128)S(1)} %get-tuple-element.4.states_ref, f32[1,1,8,8,8,128]{5,4,3,2,1,0:T(8,128)S(1)} %get-tuple-element.5.residual_ref), custom_call_target="tpu_custom_call" | custom-call | tf_op jit(solution)/shard_map/flush/pallas_call | solution.py:672

commit v7 on v6

--- a/solution.py
+++ b/solution.py
@@ -202,13 +202,13 @@
 
     for tap in range(TAPS):
         own_load(tap).wait()
+    pl.when(both(has_next, waits_loads))(first_hop.start)
     send_extra(last - 1)
     inputs_load.wait()
     bias_load.wait()
     for layer in range(1, depth):
         for index in range(len(parts)):
             fine_load(layer, index).wait()
-    pl.when(both(has_next, waits_loads))(first_hop.start)
     send_extra(last)
 
     def let_pass():
@@ -283,6 +283,7 @@
     corner_out[...] = cur[...]
     pl.when(has_next)(second_hop.start)
     pass_extra(last)
+    pass_extra(last - 1)
     pass_w(0, (1, 0))
     pass_w(1, (0,))
     pass_w(2, (0,))
@@ -317,7 +318,6 @@
         second_hop.wait_recv()
         pl.when(both(later, pos == 1))(w_ahead.start)
         send_back((3,))
-        pass_extra(last - 1)
         head[...] = next_head[...]
         cur[...] = next_head[...]
 
@@ -348,7 +348,6 @@
     pl.when(both(later, both(pos > 0, pos < last)))(g_back.start)
     pass_w(2, (1,))
     pass_w(3, (0,))
-    pass_w(0, (2,))
 
 
     for q in range(last):
@@ -356,6 +355,8 @@
         def _(q=q):
             y_copy(q).wait_recv()
             sib_copy(q).start()
+
+    pass_w(0, (2,))
 
     ends_later = both(is_last_pos, later)
     def own_step():

time: 45.9 us -> 45.8 us (level)
  no operation moved by 1% of the time
where the time goes in v7:
time: 45.8 us; the launch traced here: 45.7 us
  Pallas kernels  45 us (98%)
  between operations  0.64 us (1%)
    pallas_call x1, Pallas kernels, shards(): pl.pallas_call(body, name='mgrit_cycle', out_shape=(pltpu.VMEM(guess_stat...  44 us
    pallas_call x1, Pallas kernels, shards(): pl.pallas_call(flush, name='flush', out_shape=tuple((jax.ShapeDtypeStruct...  1.07 us

profile of v7, /device:TPU:27, one launch (start us, length us, event | category | flops | bytes accessed | tf_op | source)
XLA Modules:
  0.0 45.7 jit_solution(9934375643651685155)
XLA Ops:
  0.6 44.0 %mgrit_cycle.1 = (f32[4,1,8,8,8,128]{5,4,3,2,1,0:T(8,128)S(1)}, f32[1,1,8,8,8,128]{5,4,3,2,1,0:T(8,128)S(1)}) custom-call(f32[8,8,8,128]{3,2,1,0:T(8,128)} %bitcast.4, f32[4,1,8,8,8,128]{5,4,3,2,1,0:T(8,128)} %refs_1_.1, bf16[4,3,1152,128]{3,2,1,0:T(8,128)(2,1)} %bitcast.3, f32[4,1,1,128]{3,2,1,0:T(1,128)} %bitcast.5), custom_call_target="tpu_custom_call" | custom-call | tf_op jit(solution)/shard_map/mgrit_cycle/pallas_call | solution.py:636
  44.6 1.1 %flush.1 = (f32[4,1,8,8,8,128]{5,4,3,2,1,0:T(8,128)}, f32[1,1,8,8,8,128]{5,4,3,2,1,0:T(8,128)}) custom-call(f32[4,1,8,8,8,128]{5,4,3,2,1,0:T(8,128)S(1)} %get-tuple-element.4.states_ref, f32[1,1,8,8,8,128]{5,4,3,2,1,0:T(8,128)S(1)} %get-tuple-element.5.residual_ref), custom_call_target="tpu_custom_call" | custom-call | tf_op jit(solution)/shard_map/flush/pallas_call | solution.py:673

commit v8 on v7

--- a/solution.py
+++ b/solution.py
@@ -183,7 +183,7 @@
             pl.when(both(later, pos == source))(w_back.start)
 
     def holds(q):
-        return both(later, either(pos > q, pos == 0))
+        return both(later, either(pos > q, both(pos == 0, q < last - 1)))
 
     def first_wave():
         send_w(0, (2, 1))
@@ -317,7 +317,6 @@
     def _():
         second_hop.wait_recv()
         pl.when(both(later, pos == 1))(w_ahead.start)
-        send_back((3,))
         head[...] = next_head[...]
         cur[...] = next_head[...]
 
@@ -356,7 +355,6 @@
             y_copy(q).wait_recv()
             sib_copy(q).start()
 
-    pass_w(0, (2,))
 
     ends_later = both(is_last_pos, later)
     def own_step():
@@ -446,31 +444,19 @@
             sib_copy(turn - 1).wait_recv()
             mixed = mix(state, lead_w.at[turn - 1])
 
-            @pl.when(turn == last - 1)
-            def _():
-                y_copy(last - 1).wait_recv()
-                sib_copy(last - 1).start()
-
-            after = state + coarse_size * mixed
-
-            @pl.when(turn < last)
-            def _():
-                g_arrival(turn).wait_recv()
-                cur[...] = after + defects[turn]
-
-            @pl.when(turn == last)
-            def _():
-                c_point[...] = after
-
+            g_arrival(turn).wait_recv()
+            cur[...] = state + coarse_size * mixed + defects[turn]
             return carry
 
-        lax.fori_loop(1, COARSEN, step, 0)
+        lax.fori_loop(1, last, step, 0)
+        c_point[...] = cur[...]
         point_copy.start()
 
     @pl.when(both(ends_later, has_group_after))
     def _():
         point_copy.wait_recv()
-        c_point[...] = seed_in[...] + defects[last]
+        cur[...] = seed_in[...]
+        c_point[...] = own_step()
         start_copy.start()
 
     has_start = both(is_last_pos, group > 1)
@@ -547,9 +533,11 @@
     @pl.when(both(ends_later, jnp.logical_not(has_group_after)))
     def _():
         point_copy.wait_recv()
+        cur[...] = seed_in[...]
+        c_point[...] = own_step()
 
     corner = residual_ref[0, 0]
-    residual_ref[0, 0] = corner - jnp.where(ends_later, seed_in[...] + defects[last], corner)
+    residual_ref[0, 0] = corner - jnp.where(ends_later, c_point[...], corner)
 
     hands_on = both(both(opening, pos == 1), core == 0)
 
@@ -605,7 +593,7 @@
 
     @pl.when(both(later, pos > 0))
     def _():
-        w_back.wait_send()
+        pl.when(pos < last)(w_back.wait_send)
         pl.when(pos < last)(g_back.wait_send)
 
     @pl.when(relaxes)

time: 45.8 us -> 48.2 us (1.052)
  Pallas kernels: 45 us -> 47.4 us
    pallas_call x1, Pallas kernels: 44 us -> 46.4 us  [shards(): pl.pallas_call(body, name='mgrit_cycle', out_shape=(pltpu.VMEM(guess_stat...]
where the time goes in v8:
time: 48.2 us; the launch traced here: 48.1 us
  Pallas kernels  47.4 us (98%)
  between operations  0.64 us (1%)
    pallas_call x1, Pallas kernels, shards(): pl.pallas_call(body, name='mgrit_cycle', out_shape=(pltpu.VMEM(guess_stat...  46.4 us
    pallas_call x1, Pallas kernels, shards(): pl.pallas_call(flush, name='flush', out_shape=tuple((jax.ShapeDtypeStruct...  1.07 us

profile of v8, /device:TPU:27, one launch (start us, length us, event | category | flops | bytes accessed | tf_op | source)
XLA Modules:
  0.0 48.1 jit_solution(8465468646551414523)
XLA Ops:
  0.6 46.4 %mgrit_cycle.1 = (f32[4,1,8,8,8,128]{5,4,3,2,1,0:T(8,128)S(1)}, f32[1,1,8,8,8,128]{5,4,3,2,1,0:T(8,128)S(1)}) custom-call(f32[8,8,8,128]{3,2,1,0:T(8,128)} %bitcast.4, f32[4,1,8,8,8,128]{5,4,3,2,1,0:T(8,128)} %refs_1_.1, bf16[4,3,1152,128]{3,2,1,0:T(8,128)(2,1)} %bitcast.3, f32[4,1,1,128]{3,2,1,0:T(1,128)} %bitcast.5), custom_call_target="tpu_custom_call" | custom-call | tf_op jit(solution)/shard_map/mgrit_cycle/pallas_call | solution.py:624
  47.0 1.1 %flush.1 = (f32[4,1,8,8,8,128]{5,4,3,2,1,0:T(8,128)}, f32[1,1,8,8,8,128]{5,4,3,2,1,0:T(8,128)}) custom-call(f32[4,1,8,8,8,128]{5,4,3,2,1,0:T(8,128)S(1)} %get-tuple-element.4.states_ref, f32[1,1,8,8,8,128]{5,4,3,2,1,0:T(8,128)S(1)} %get-tuple-element.5.residual_ref), custom_call_target="tpu_custom_call" | custom-call | tf_op jit(solution)/shard_map/flush/pallas_call | solution.py:661
